TPU v7x, 32 devices: a whole 2x2x4 slice. The times are simulated.
32 devices in a mesh: gx: 2 (over y), gy: 4 (over x, core), gz: 4 (over z).
Axes of the slice: x: 2, y: 2, z: 4, core: 2. Of those that a mesh axis runs over, the one named last changes fastest.
Arguments:
- fluid_state: float32 [4, 32, 64, 512], P(None, 'gx', 'gy', 'gz'), may hold values from -6 to 6
- shell_disp: float32 [3, 32768], P(None, ('gy', 'gz')), may hold values from -6 to 6
- quad_weights: float32 [32, 32, 64], P(('gx', 'gy', 'gz')), may hold values from 0.25 to 1
- quad_elements: int32 [32, 32, 64], P(('gx', 'gy', 'gz')), may hold values from 0 to 32767
- owner_cells: int32 [32, 32, 64], P(('gx', 'gy', 'gz')), may hold values from 0 to 32767
- owner_counts: int32 [32, 32], P(('gx', 'gy', 'gz')), may hold values from 0 to 64, as said below
Outputs:
- fluid_out: float32 [4, 32, 64, 512], P(None, 'gx', 'gy', 'gz')
- shell_out: float32 [3, 32768], P(None, ('gy', 'gz'))
Inputs may be any that keep to these rules, and one draw needn't show every extreme that they name: `owner_counts`: some owner has 64 live records from every sender; some owner has none from some sender.
All inputs are finite; a program needn't handle non-finite values.
Results may differ from a plain program's by a relative error of at most 0.000023.
Values sent between devices are 32-bit elements; how exact they have to be, the bound alone decides.
A program may use at most 128 MiB of HBM per device.

v0:
```python
import jax
import jax.numpy as jnp
from jax import lax
from jax.sharding import PartitionSpec as P

ITERS = 2


advection = 0.2
penalty = 0.5
relaxation = 0.05


def with_halo(cells, sides, width):
    for axis, dim in sides:
        count = lax.axis_size(axis)
        ends = count - 1
        head = lax.slice_in_dim(cells, 0, width, axis=dim)
        tail = lax.slice_in_dim(cells, cells.shape[dim] - width, cells.shape[dim], axis=dim)
        cells = jnp.concatenate(
            [
                lax.ppermute(tail, axis, [(i, (i + 1) % count) for i in range(ends)]),
                cells,
                lax.ppermute(head, axis, [((i + 1) % count, i) for i in range(ends)]),
            ],
            axis=dim,
        )
    return cells


def smooth_axis(values, axis):
    length = values.shape[axis] - 2
    lower = lax.slice_in_dim(values, 0, length, axis=axis)
    middle = lax.slice_in_dim(values, 1, length + 1, axis=axis)
    upper = lax.slice_in_dim(values, 2, length + 2, axis=axis)
    return 0.25 * lower + 0.5 * middle + 0.25 * upper


def sweep_fluid(padded):
    smoothed = smooth_axis(smooth_axis(smooth_axis(padded, 1), 2), 3)
    center = padded[:, 1:-1, 1:-1, 1:-1]
    grad_x = 0.5 * (padded[:, 2:, 1:-1, 1:-1] - padded[:, :-2, 1:-1, 1:-1])
    grad_y = 0.5 * (padded[:, 1:-1, 2:, 1:-1] - padded[:, 1:-1, :-2, 1:-1])
    grad_z = 0.5 * (padded[:, 1:-1, 1:-1, 2:] - padded[:, 1:-1, 1:-1, :-2])
    convect = center[0:1] * grad_x + center[1:2] * grad_y + center[2:3] * grad_z
    updated = smoothed - advection * convect
    pressure_grad = jnp.stack([grad_x[3], grad_y[3], grad_z[3]])
    return jnp.concatenate([updated[0:3] - advection * pressure_grad, updated[3:4]], 0)


def on_device(fluid_state, shell_disp, quad_weights, quad_elements, owner_cells, owner_counts):
    slots = quad_weights.shape[2]
    elements = quad_elements[0]
    cells_local = owner_cells[0]
    slot_index = jnp.arange(slots, dtype=jnp.int32)[None, :]
    live_mask = (slot_index < owner_counts[0][:, None]).astype(jnp.float32)
    block_shape = fluid_state.shape
    for iteration in range(ITERS):
        padded = with_halo(fluid_state, (("gx", 1), ("gy", 2), ("gz", 3)), 1)
        halfway = sweep_fluid(padded)
        all_nodes = lax.all_gather(shell_disp, ("gy", "gz"), axis=1, tiled=True)
        shell_vel = all_nodes[:, elements]
        records = jnp.concatenate([shell_vel, quad_weights[0][None]], 0)
        received = lax.all_to_all(
            records, ("gx", "gy", "gz"), split_axis=1, concat_axis=1, tiled=True
        )
        flat_vel = halfway[0:3].reshape(3, -1)
        velocity = flat_vel[:, cells_local]
        traction = penalty * received[3][None] * (velocity - received[0:3]) * live_mask[None]
        forcing = jnp.zeros_like(flat_vel).at[:, cells_local].add(traction)
        forcing = forcing.reshape(3, block_shape[1], block_shape[2], block_shape[3])
        fluid_state = jnp.concatenate([halfway[0:3] - forcing, halfway[3:4]], 0)
        returned = lax.all_to_all(
            traction, ("gx", "gy", "gz"), split_axis=1, concat_axis=1, tiled=True
        )
        node_terms = jnp.zeros((3, all_nodes.shape[1]), jnp.float32).at[:, elements].add(returned)
        partial_loads = lax.psum_scatter(node_terms, ("gy", "gz"), scatter_dimension=1, tiled=True)
        node_loads = lax.psum(partial_loads, "gx")
        shell_disp = shell_disp + relaxation * node_loads
    return (fluid_state, shell_disp)


def solution(mesh):
    return jax.shard_map(
        on_device,
        mesh=mesh,
        in_specs=(
            P(None, "gx", "gy", "gz"),
            P(None, ("gy", "gz")),
            P(("gx", "gy", "gz"), None, None),
            P(("gx", "gy", "gz"), None, None),
            P(("gx", "gy", "gz"), None, None),
            P(("gx", "gy", "gz"), None),
        ),
        out_specs=(P(None, "gx", "gy", "gz"), P(None, ("gy", "gz"))),
        check_vma=False,
    )
```

profile of v0, /device:TPU:0, one launch (start us, length us, event | category | flops | bytes accessed | tf_op | source)
XLA Modules:
  0.0 1414.3 jit_solution(13298228462873777052)
XLA Ops:
  16.1 359.1 %all_gather.6 = f32[3,32768]{0,1:T(8,128)} all-gather(f32[3,2048]{0,1:T(8,128)S(1)} %copy.153), channel_id=1, replica_groups=mesh['gx'=2,'gy'=4,'gz'=4] {'gy','gz'}, dimensions={1}, use_global_device_ids=true | all-gather | bytes 417792 | tf_op jit(solution)/shard_map/all_gather | solution.py:61
  375.3 11.2 gather_fusion
  387.7 5.4 all-to-all-start
  412.5 8.1 pad_maximum_fusion
  444.0 8.7 copy.157
  452.7 13.3 gather_fusion.1
  469.1 18.6 %scatter_custom_fusion = f32[3,32768]{0,1:T(8,128)} fusion(s32[2048]{0:T(1024)} %copy-done.35, f32[2048,3]{1,0:T(8,128)} %bitcast.86, f32[]{:T(128)} %constant.10.clone.1), kind=kCustom, calls=%fused_computation.14 | custom fusion | flops 6144 | bytes 393728 | tf_op jit(solution)/shard_map/scatter-add | solution.py:70
  487.7 10.0 copy.161
  503.2 10.1 all-to-all-start.1
  531.6 8.1 pad_maximum_fusion.1
  548.6 18.6 %scatter_custom_fusion.1 = f32[3,32768]{0,1:T(8,128)} fusion(s32[2048]{0:T(1024)} %copy-done.34, f32[2048,3]{1,0:T(8,128)} %bitcast.87, f32[]{:T(128)} %constant.10.clone.1), kind=kCustom, calls=%fused_computation.12 | custom fusion | flops 6144 | bytes 393728 | tf_op jit(solution)/shard_map/scatter-add | solution.py:76
  580.8 168.3 %reduce-scatter.3.cloned.1.call-done = f32[3,2048]{0,1:T(8,128)} async-done(((f32[3,32768]{0,1:T(8,128)}), f32[3,2048]{0,1:T(8,128)}) %reduce-scatter.3.cloned.1.call-update) | async-done | bytes 24592 | tf_op jit(solution)/shard_map/reduce_scatter | solution.py:77
  749.1 28.5 %psum.14 = f32[3,2048]{0,1:T(8,128)S(1)} all-reduce(f32[3,2048]{0,1:T(8,128)} %reduce-scatter.3.cloned.1.call-done), channel_id=1, replica_groups=mesh['gx'=2,'gy'=4,'gz'=4] {'gx'}, use_global_device_ids=true, to_apply=%region_3.0 | all-reduce | flops 6144 | bytes 49152 | tf_op jit(solution)/shard_map/psum | solution.py:78
  777.7 353.5 %all_gather.7 = f32[3,32768]{0,1:T(8,128)} all-gather(f32[3,2048]{0,1:T(8,128)S(1)} %multiply_add_fusion.1), channel_id=1, replica_groups=mesh['gx'=2,'gy'=4,'gz'=4] {'gy','gz'}, dimensions={1}, use_global_device_ids=true | all-gather | bytes 417792 | tf_op jit(solution)/shard_map/all_gather | solution.py:61
  1131.2 11.2 gather_fusion.2
  1148.9 8.7 copy.182
  1157.6 11.2 gather_fusion.3
  1170.8 5.8 all-to-all-start.3
  1176.8 7.2 all-to-all-done.3
  1185.3 18.4 %scatter_custom_fusion.3 = f32[3,32768]{0,1:T(8,128)} fusion(s32[2048]{0:T(1024)} %copy-done.34, f32[2048,3]{1,0:T(8,128)S(1)} %bitcast.85, f32[]{:T(128)} %constant.10.clone.1), kind=kCustom, calls=%fused_computation.8 | custom fusion | flops 6144 | bytes 393728 | tf_op jit(solution)/shard_map/scatter-add | solution.py:76
  1204.1 21.6 %scatter_custom_fusion.2 = f32[3,32768]{0,1:T(8,128)} fusion(s32[2048]{0:T(1024)} %copy-done.35, f32[2048,3]{1,0:T(8,128)S(1)} %bitcast.84, f32[]{:T(128)} %constant.10.clone.1), kind=kCustom, calls=%fused_computation.10 | custom fusion | flops 6144 | bytes 393728 | tf_op jit(solution)/shard_map/scatter-add | solution.py:70
  1225.7 10.3 copy.186
  1236.9 140.6 %reduce-scatter.5.cloned.1.call-done = f32[3,2048]{0,1:T(8,128)} async-done(((f32[3,32768]{0,1:T(8,128)}), f32[3,2048]{0,1:T(8,128)}) %reduce-scatter.5.cloned.1.call-update) | async-done | bytes 24592 | tf_op jit(solution)/shard_map/reduce_scatter | solution.py:77
  1377.5 28.5 %psum.15 = f32[3,2048]{0,1:T(8,128)S(1)} all-reduce(f32[3,2048]{0,1:T(8,128)} %reduce-scatter.5.cloned.1.call-done), channel_id=1, replica_groups=mesh['gx'=2,'gy'=4,'gz'=4] {'gx'}, use_global_device_ids=true, to_apply=%region_7.0 | all-reduce | flops 6144 | bytes 49152 | tf_op jit(solution)/shard_map/psum | solution.py:78
  (204 shorter events, 113.8 us)
Async XLA Ops:
  8.0 386.0 %collective-permute-start = (f32[4,1,16,128]{3,2,1,0:T(8,128)S(1)}, f32[4,1,16,128]{3,2,1,0:T(8,128)S(1)}, u32[]{:S(2)}, u32[]{:S(2)}) collective-permute-start(f32[4,1,16,128]{3,2,1,0:T(8,128)S(1)} %get-tuple-element.36), channel_id=1, source_target_pairs={{0,16},{1,17},{2,18},{3,19},{4,20},{5,21},{6,22},{7,23},{8,24},{9,... | collective-permute-start | bytes 98312 | tf_op jit(solution)/shard_map/ppermute | solution.py:22
  12.8 381.2 %collective-permute-start.1 = (f32[4,1,16,128]{3,2,1,0:T(8,128)S(1)}, f32[4,1,16,128]{3,2,1,0:T(8,128)S(1)}, u32[]{:S(2)}, u32[]{:S(2)}) collective-permute-start(f32[4,1,16,128]{3,2,1,0:T(8,128)S(1)} %get-tuple-element.35), channel_id=1, source_target_pairs={{16,0},{17,1},{18,2},{19,3},{20,4},{21,5},{22,6},{23,7},{24,8},{25... | collective-permute-start | bytes 98312 | tf_op jit(solution)/shard_map/ppermute | solution.py:24
  16.1 370.8 %copy-start.32 = (f32[1,32,64]{2,1,0:T(8,128)S(1)}, f32[1,32,64]{2,1,0:T(8,128)}, u32[]{:S(2)}) copy-start(f32[1,32,64]{2,1,0:T(8,128)} %param.8) | copy-start | bytes 24580
  16.1 377.0 %copy-start.5 = (f32[4,16,16,128]{3,2,1,0:T(8,128)S(1)}, f32[4,16,16,128]{3,2,1,0:T(8,128)}, u32[]{:S(2)}) copy-start(f32[4,16,16,128]{3,2,1,0:T(8,128)} %param.6) | copy-start | bytes 1572868
  16.1 377.7 %copy-start.36 = (s32[1,32,64]{2,1,0:T(8,128)S(1)}, s32[1,32,64]{2,1,0:T(8,128)}, u32[]{:S(2)}) copy-start(s32[1,32,64]{2,1,0:T(8,128)} %param.10) | copy-start | bytes 24580
  16.1 377.7 %copy-start.37 = (s32[1,32]{1,0:T(1,128)S(1)}, s32[1,32]{1,0:T(1,128)}, u32[]{:S(2)}) copy-start(s32[1,32]{1,0:T(1,128)} %param.11) | copy-start | bytes 388
  387.7 14.7 %all-to-all-start = ((f32[32,1,256]{2,1,0:T(1,128)}), f32[32,1,256]{2,1,0:T(1,128)S(1)}, u32[]{:S(2)}, u32[]{:S(2)}) async-start(f32[32,1,256]{2,1,0:T(1,128)} %reshape.189), calls=%async_computation | async-start | bytes 65536 | tf_op jit(solution)/shard_map/all_to_all | solution.py:64
  394.7 9.2 collective-permute-start.2
  396.9 11.2 collective-permute-start.3
  423.9 11.5 collective-permute-start.4
  428.0 8.7 collective-permute-start.5
  497.8 15.6 %collective-permute-start.6 = (f32[4,1,16,128]{3,2,1,0:T(8,128)S(1)}, f32[4,1,16,128]{3,2,1,0:T(8,128)S(1)}, u32[]{:S(2)}, u32[]{:S(2)}) collective-permute-start(f32[4,1,16,128]{3,2,1,0:T(8,128)S(1)} %get-tuple-element.30), channel_id=1, source_target_pairs={{0,16},{1,17},{2,18},{3,19},{4,20},{5,21},{6,22},{7,23},{8,24},{9,... | collective-permute-start | bytes 98312 | tf_op jit(solution)/shard_map/ppermute | solution.py:22
  501.2 12.3 collective-permute-start.7
  503.2 19.0 %all-to-all-start.1 = ((f32[32,1,192]{2,1,0:T(1,128)}), f32[32,1,192]{2,1,0:T(1,128)S(1)}, u32[]{:S(2)}, u32[]{:S(2)}) async-start(f32[32,1,192]{2,1,0:T(1,128)} %reshape.191), calls=%async_computation.1 | async-start | bytes 65536 | tf_op jit(solution)/shard_map/all_to_all | solution.py:73
  513.4 235.7 %reduce-scatter.3.cloned.1.call-start = ((), (), s32[]{:S(2)}) async-start(), calls=%async_computation.6 | async-start | bytes 17825792 | tf_op jit(solution)/shard_map/reduce_scatter | solution.py:77
  514.2 8.9 collective-permute-start.8
  516.4 11.0 collective-permute-start.9
  542.4 30.2 %collective-permute-start.10 = (f32[4,18,18,1]{2,1,3,0:T(8,128)S(1)}, f32[4,18,18,1]{2,1,3,0:T(8,128)S(1)}, u32[]{:S(2)}, u32[]{:S(2)}) collective-permute-start(f32[4,18,18,1]{2,1,3,0:T(8,128)S(1)} %get-tuple-element.22), channel_id=1, source_target_pairs={{0,1},{1,2},{2,3},{4,5},{5,6},{6,7},{8,9},{9,10},{10,11},{12,13},{... | collective-permute-start | bytes 15560 | tf_op jit(solution)/shard_map/ppermute | solution.py:22
  545.9 28.1 %collective-permute-start.11 = (f32[4,18,18,1]{2,1,3,0:T(8,128)S(1)}, f32[4,18,18,1]{2,1,3,0:T(8,128)S(1)}, u32[]{:S(2)}, u32[]{:S(2)}) collective-permute-start(f32[4,18,18,1]{2,1,3,0:T(8,128)S(1)} %get-tuple-element.23), channel_id=1, source_target_pairs={{1,0},{2,1},{3,2},{5,4},{6,5},{7,6},{9,8},{10,9},{11,10},{13,12},{... | collective-permute-start | bytes 15560 | tf_op jit(solution)/shard_map/ppermute | solution.py:24
  777.7 365.2 %copy-start.33 = (f32[1,32,64]{2,1,0:T(8,128)S(1)}, f32[1,32,64]{2,1,0:T(8,128)}, u32[]{:S(2)}) copy-start(f32[1,32,64]{2,1,0:T(8,128)} %param.8) | copy-start | bytes 24580
  777.7 371.1 %copy-start.6 = (f32[4,16,16,128]{3,2,1,0:T(8,128)S(1)}, f32[4,16,16,128]{3,2,1,0:T(8,128)}, u32[]{:S(2)}) copy-start(f32[4,16,16,128]{3,2,1,0:T(8,128)} %get-tuple-element.14) | copy-start | bytes 1572868
  1143.6 25.6 %all-to-all-start.2 = ((f32[32,1,256]{2,1,0:T(1,128)}), f32[32,1,256]{2,1,0:T(1,128)S(1)}, u32[]{:S(2)}, u32[]{:S(2)}) async-start(f32[32,1,256]{2,1,0:T(1,128)} %reshape.193), calls=%async_computation.3 | async-start | bytes 65536 | tf_op jit(solution)/shard_map/all_to_all | solution.py:64
  1170.8 13.1 all-to-all-start.3
  1176.7 200.8 %reduce-scatter.5.cloned.1.call-start = ((), (), s32[]{:S(2)}) async-start(), calls=%async_computation.7 | async-start | bytes 17825792 | tf_op jit(solution)/shard_map/reduce_scatter | solution.py:77
  (32 other events, 1260.1 us)
Sparse Core Ops, SparseCore 0:
  567.3 181.6 reduce-scatter.2
  1203.8 173.6 reduce-scatter.4
where the time goes:
time: 1420 us; the launch traced here: 1410 us
  blocking collectives  770 us (54%)
  waiting for transfers between devices  316 us (22%)
  local copies, waits for them, and re-layouts  151 us (11%)
  other arithmetic  107 us (8%)
  starting transfers between devices  55 us (4%)
  between operations  15.5 us (1%)
    all_gather x2, blocking collectives, on_device(): all_nodes = lax.all_gather(shell_disp, ('gy', 'gz'), axis=1, tiled=True)  713 us
    reduce_scatter x2, waiting for transfers between devices, on_device(): lax.psum_scatter(node_terms, ('gy', 'gz'), scatter_dimension=1, tiled=True)  309 us
    psum x2, blocking collectives, on_device(): node_loads = lax.psum(partial_loads, 'gx')  56.9 us
    scatter-add x2, other arithmetic, on_device(): forcing = jnp.zeros_like(flat_vel).at[:, cells_local].add(traction)  40.2 us
    scatter-add x2, other arithmetic, on_device(): jnp.zeros((3, all_nodes.shape[1]), jnp.float32).at[:, elements]  37 us
  transfers between devices with their start and end apart: 18, of which 3 were waited for; matrix products, arithmetic and copies ran while one was open for 9% of the time, Pallas kernels for 0%

commit v1 on v0

v1 whole, which is shorter than its diff:
```python
import functools

import jax
import jax.numpy as jnp
from jax import lax
from jax.experimental import pallas as pl
from jax.experimental.pallas import tpu as pltpu
from jax.sharding import PartitionSpec as P

ITERS = 2

advection = 0.2
penalty = 0.5
relaxation = 0.05
AXES = ("gx", "gy", "gz")
MESH = pl.DeviceIdType.MESH
F32 = jnp.float32
BF16 = jnp.bfloat16


class Place:
    def __init__(self, sizes):
        self.nx, self.ny, self.nz = sizes
        self.plane = self.nx * self.ny
        self.x, self.y, self.z = (lax.axis_index(a) for a in AXES)
        self.p = self.x * self.ny + self.y

    def plane_peer(self, d):
        p = lax.rem(self.p + d, self.plane)
        return p, (lax.div(p, self.ny), lax.rem(p, self.ny), self.z)

    def line_peer(self, d):
        z = lax.rem(self.z + d, self.nz)
        return z, (self.x, self.y, z)

    def barrier(self):
        sem = pltpu.get_barrier_semaphore()
        for d in range(1, self.plane):
            pl.semaphore_signal(sem, inc=1, device_id=self.plane_peer(d)[1], device_id_type=MESH)
        for d in range(1, self.nz):
            pl.semaphore_signal(sem, inc=1, device_id=self.line_peer(d)[1], device_id_type=MESH)
        pl.semaphore_wait(sem, self.plane - 1 + self.nz - 1)


def send(src, dst, sems, k, device):
    return pltpu.make_async_remote_copy(
        src_ref=src, dst_ref=dst, send_sem=sems.at[0, k], recv_sem=sems.at[1, k],
        device_id=device, device_id_type=MESH,
    )


def start_all(copies):
    for c in copies:
        c.start()
    return copies


def wait_all(copies):
    for c in copies:
        c.wait()


class Halo:
    def __init__(self, here, count, device_of, srcs, dsts, sems):
        self.has = (here > 0, here < count - 1)
        self.copies = []
        for s in (0, 1):
            there = jnp.clip(here + (2 * s - 1), 0, count - 1)
            self.copies.append(send(srcs[s], dsts[1 - s], sems, s, device_of(there)))

    def start(self):
        for s in (0, 1):
            @pl.when(self.has[s])
            def _():
                self.copies[s].start()

    def wait(self):
        for s in (0, 1):
            @pl.when(self.has[s])
            def _():
                self.copies[s].wait_send()
                self.copies[1 - s].wait_recv()


class Sweep:
    def __init__(self, at, f, half, fx, sx, sxy, ys, yh, zs, zh, sem_x, sem_y, sem_z):
        self.at, self.f, self.half, self.fx, self.sx, self.sxy = at, f, half, fx, sx, sxy
        self.ys, self.yh, self.zs, self.zh = ys, yh, zs, zh
        self.nf, self.bx, self.by, self.bz = f.shape
        bx = self.bx
        self.hx = Halo(at.x, at.nx, lambda x: (x, at.y, at.z),
                       (f.at[:, 0], f.at[:, bx - 1]), (fx.at[:, 0], fx.at[:, bx + 1]), sem_x)
        self.hy = Halo(at.y, at.ny, lambda y: (at.x, y, at.z),
                       (ys.at[0], ys.at[1]), (yh.at[0], yh.at[1]), sem_y)
        self.hz = Halo(at.z, at.nz, lambda z: (at.x, at.y, z),
                       (zs.at[0], zs.at[1]), (zh.at[0], zh.at[1]), sem_z)

    def start_x(self):
        self.hx.start()
        for s, edge in ((0, 0), (1, self.bx + 1)):
            @pl.when(jnp.logical_not(self.hx.has[s]))
            def _():
                self.fx[:, edge] = jnp.zeros((self.nf, self.by, self.bz), F32)

            @pl.when(jnp.logical_not(self.hy.has[s]))
            def _():
                self.yh[s] = jnp.zeros(self.yh.shape[1:], F32)

            @pl.when(jnp.logical_not(self.hz.has[s]))
            def _():
                self.zh[s] = jnp.zeros(self.zh.shape[1:], F32)
        self.fx[:, 1:self.bx + 1] = self.f[...]

    def x_then_start_y(self):
        self.hx.wait()

        def step(x, _):
            for c in range(self.nf):
                mid = self.fx[c, x + 1]
                s = 0.25 * self.fx[c, x] + 0.5 * mid + 0.25 * self.fx[c, x + 2]
                self.sx[c, x] = s
                row = c * self.bx + x
                self.ys[0, 0, pl.ds(row, 1), :] = mid[0:1]
                self.ys[1, 0, pl.ds(row, 1), :] = mid[self.by - 1:]
                self.ys[0, 1, pl.ds(row, 1), :] = s[0:1]
                self.ys[1, 1, pl.ds(row, 1), :] = s[self.by - 1:]
            return 0

        lax.fori_loop(0, self.bx, step, 0)
        self.hy.start()

    def shift_y(self, tile, c, x, kind):
        sub = lax.broadcasted_iota(jnp.int32, tile.shape, 0)
        row = c * self.bx + x
        lower = jnp.where(sub == 0, self.yh[0, kind, pl.ds(row, 1), :], pltpu.roll(tile, 1, axis=0))
        upper = jnp.where(sub == self.by - 1, self.yh[1, kind, pl.ds(row, 1), :],
                          pltpu.roll(tile, self.by - 1, axis=0))
        return lower, upper

    def y_then_start_z(self):
        self.hy.wait()
        lane = lax.broadcasted_iota(jnp.int32, (self.by, self.zs.shape[2]), 1)
        group = self.nf * self.bx

        def step(x, faces):
            low, high = faces
            for c in range(self.nf):
                tile = self.sx[c, x]
                lower, upper = self.shift_y(tile, c, x, 1)
                s = 0.25 * lower + 0.5 * tile + 0.25 * upper
                self.sxy[c, x] = s
                raw = self.fx[c, x + 1]
                k = c * self.bx + x
                low = jnp.where(lane == k, raw[:, 0:1], low)
                low = jnp.where(lane == k + group, s[:, 0:1], low)
                high = jnp.where(lane == k, raw[:, self.bz - 1:], high)
                high = jnp.where(lane == k + group, s[:, self.bz - 1:], high)
            return low, high

        zero = jnp.zeros(lane.shape, F32)
        low, high = lax.fori_loop(0, self.bx, step, (zero, zero))
        self.zs[0] = low
        self.zs[1] = high
        self.hz.start()

    def finish(self):
        self.hz.wait()
        lane = lax.broadcasted_iota(jnp.int32, (self.by, self.bz), 1)
        width = self.zs.shape[2]
        group = self.nf * self.bx

        def step(x, _):
            turn = lax.rem(width - x, width)
            low, high = (pltpu.roll(self.zh[s], turn, axis=1) for s in (0, 1))

            def shift_z(tile, k):
                lower = jnp.where(lane == 0, low[:, k:k + 1], pltpu.roll(tile, 1, axis=1))
                upper = jnp.where(lane == self.bz - 1, high[:, k:k + 1], pltpu.roll(tile, self.bz - 1, axis=1))
                return lower, upper

            u = [self.fx[c, x + 1] for c in range(3)]
            for c in range(self.nf):
                raw = self.fx[c, x + 1]
                s = self.sxy[c, x]
                lower, upper = shift_z(s, group + c * self.bx)
                smoothed = 0.25 * lower + 0.5 * s + 0.25 * upper
                grad_x = 0.5 * (self.fx[c, x + 2] - self.fx[c, x])
                lower, upper = self.shift_y(raw, c, x, 0)
                grad_y = 0.5 * (upper - lower)
                lower, upper = shift_z(raw, c * self.bx)
                grad_z = 0.5 * (upper - lower)
                self.half[c, x] = smoothed - advection * (u[0] * grad_x + u[1] * grad_y + u[2] * grad_z)
                if c == 3:
                    for v, g in enumerate((grad_x, grad_y, grad_z)):
                        self.half[v, x] = self.half[v, x] - advection * g
            return 0

        lax.fori_loop(0, self.bx, step, 0)


def sweep_scratch(block):
    nf, bx, by, bz = block
    width = -(-2 * nf * bx // 128) * 128
    dma = pltpu.SemaphoreType.DMA((2, 2))
    return [
        pltpu.VMEM((nf, bx + 2, by, bz), F32), pltpu.VMEM(block, F32), pltpu.VMEM(block, F32),
        pltpu.VMEM((2, 2, nf * bx, bz), F32), pltpu.VMEM((2, 2, nf * bx, bz), F32),
        pltpu.VMEM((2, by, width), F32), pltpu.VMEM((2, by, width), F32), dma, dma, dma,
    ]


def gather_line(at, piece, line, sems):
    return start_all([send(piece, line.at[at.z], sems, d - 1, at.line_peer(d)[1]) for d in range(1, at.nz)])


def gather_plane(at, line, nodes, sems):
    return start_all([send(line, nodes.at[at.p], sems, d - 1, at.plane_peer(d)[1]) for d in range(1, at.plane)])


def first_kernel(sizes, f, shell, rec, half, nodes, records, line, rec_line,
                 sem_nl, sem_np, sem_rl, sem_rp, *sweep_refs):
    at = Place(sizes)
    sweep = Sweep(at, f, half, *sweep_refs)
    at.barrier()
    sweep.start_x()
    node_copies = gather_line(at, shell.at[at.x], line, sem_nl)
    rec_copies = []
    for d in range(1, at.nz):
        z, device = at.line_peer(d)
        rec_copies.append(send(rec.at[z], rec_line.at[at.z], sem_rl, d - 1, device))
    start_all(rec_copies)
    line[at.z] = shell[at.x]
    rec_line[at.z] = rec[at.z]
    sweep.x_then_start_y()
    wait_all(node_copies)
    node_copies = gather_plane(at, line, nodes, sem_np)
    wait_all(rec_copies)
    rec_copies = []
    for d in range(1, at.plane):
        p, device = at.plane_peer(d)
        rec_copies.append(send(rec_line.at[:, p], records.at[at.p], sem_rp, d - 1, device))
    start_all(rec_copies)
    nodes[at.p] = line[...]
    records[at.p] = rec_line[:, at.p]
    sweep.y_then_start_z()
    sweep.finish()
    wait_all(node_copies)
    wait_all(rec_copies)


def reduce_plane(at, terms, landed, sems):
    copies = []
    for d in range(1, at.plane):
        p, device = at.plane_peer(d)
        copies.append(send(terms.at[p], landed.at[d - 1], sems, d - 1, device))
    return start_all(copies)


def sum_plane(at, terms, landed, sums):
    total = terms[at.p]
    for d in range(1, at.plane):
        total = total + landed[d - 1]
    sums[...] = total


def reduce_line(at, sums, landed, sems):
    copies = []
    for d in range(1, at.nz):
        z, device = at.line_peer(d)
        copies.append(send(sums.at[z], landed.at[d - 1], sems, d - 1, device))
    return start_all(copies)


def sum_line(at, sums, landed):
    total = sums[at.z]
    for d in range(1, at.nz):
        total = total + landed[d - 1]
    return total


def middle_kernel(sizes, f, shell, terms, half, nodes, mine, landed_p, sums, landed_l, line,
                  sem_rp, sem_rl, sem_nl, sem_np, *sweep_refs):
    at = Place(sizes)
    sweep = Sweep(at, f, half, *sweep_refs)
    at.barrier()
    sweep.start_x()
    copies = reduce_plane(at, terms, landed_p, sem_rp)
    sweep.x_then_start_y()
    wait_all(copies)
    sum_plane(at, terms, landed_p, sums)
    copies = reduce_line(at, sums, landed_l, sem_rl)
    sweep.y_then_start_z()
    wait_all(copies)
    fresh = shell[at.x] + relaxation * sum_line(at, sums, landed_l)
    mine[...] = fresh
    line[at.z] = fresh
    copies = gather_line(at, mine, line, sem_nl)
    sweep.finish()
    wait_all(copies)
    copies = gather_plane(at, line, nodes, sem_np)
    nodes[at.p] = line[...]
    wait_all(copies)


def last_kernel(sizes, shell, terms, out, landed_p, sums, landed_l, mine, sem_rp, sem_rl, sem_g):
    at = Place(sizes)
    at.barrier()
    copies = reduce_plane(at, terms, landed_p, sem_rp)
    wait_all(copies)
    sum_plane(at, terms, landed_p, sums)
    copies = reduce_line(at, sums, landed_l, sem_rl)
    wait_all(copies)
    fresh = shell[...] + relaxation * sum_line(at, sums, landed_l)
    mine[...] = fresh
    copies = []
    for d in range(1, at.nx):
        x = lax.rem(at.x + d, at.nx)
        copies.append(send(mine, out.at[at.x], sem_g, d - 1, (x, at.y, at.z)))
    start_all(copies)
    out[at.x] = fresh
    wait_all(copies)


def couple_kernel(sizes, half, nodes, weights_ids, cells, live, fluid, terms, hs, ns, nf32, acc_f, acc_n):
    nx, ny, nz = sizes
    rp, lp, pr, plane_lanes = piece_split(nx, nodes.shape[3:])
    rows = acc_f.shape[0] // 3
    lanes = acc_f.shape[1]
    size = 3 * rows

    def split_store(ref, c, value):
        hi = value.astype(BF16)
        ref[c * rows:(c + 1) * rows] = hi
        ref[size + c * rows:size + (c + 1) * rows] = (value - hi.astype(F32)).astype(BF16)

    def pieces():
        for g in range(nx):
            r0, l0 = (g // lp) * pr, (g % lp) * plane_lanes
            for y in range(ny):
                for z in range(nz):
                    for c in range(3):
                        r = c * rows + (y * nz + z) * (rp * pr) + r0
                        yield g * ny + y, z, c, slice(r, r + pr), slice(l0, l0 + plane_lanes)

    for p, z, c, r, l in pieces():
        nf32[r, l] = nodes[p, z, c]
    for c in range(3):
        value = half[c]
        bx, by, bz = value.shape
        top = value[:, :by // 2].reshape(bx * by // 2, bz)
        low = value[:, by // 2:].reshape(bx * by // 2, bz)
        split_store(hs, c, jnp.concatenate([top, low], axis=1))
        split_store(ns, c, nf32[c * rows:(c + 1) * rows])
    acc_f[...] = jnp.zeros_like(acc_f)
    acc_n[...] = jnp.zeros_like(acc_n)
    width = cells.shape[1]
    sources = cells.shape[0]
    lane_of = lax.broadcasted_iota(jnp.int32, (lanes, 2 * width), 0)
    row_of = lax.broadcasted_iota(jnp.int32, (rows, 2 * width), 0)
    by, bz = half.shape[2:]
    hy = by // 2
    left = lax.broadcasted_iota(jnp.int32, (1, width), 1) < width // 2

    def chunk(q):
        def both(read):
            return jnp.concatenate([read(2 * q), read(2 * q + 1)], axis=1)

        def weight(i):
            top, bottom = weights_ids[pl.ds(i, 1), :], weights_ids[pl.ds(i + sources, 1), :]
            return jnp.where(left, top, pltpu.roll(bottom, width // 2, axis=1))

        def ident(i):
            top, bottom = weights_ids[pl.ds(i, 1), :], weights_ids[pl.ds(i + sources, 1), :]
            return jnp.where(left, pltpu.roll(top, width // 2, axis=1), bottom)

        factor = penalty * both(weight) * both(lambda i: live[pl.ds(i, 1), :])
        node = both(ident).astype(jnp.int32)
        cell = both(lambda i: cells[pl.ds(i, 1), :])
        z = lax.rem(cell, bz)
        y = lax.rem(lax.div(cell, bz), by)
        x = lax.div(cell, by * bz)
        places = (
            (hs, x * hy + lax.rem(y, hy), lax.div(y, hy) * bz + z),
            (ns, lax.div(node, lanes), lax.rem(node, lanes)),
        )
        hots, masks, values = [], [], []
        for ref, r, l in places:
            hot = jnp.where(lane_of == l, 1.0, 0.0).astype(BF16)
            mask = row_of == r
            found = jnp.dot(ref[...], hot, preferred_element_type=F32)
            found = found[:size] + found[size:]
            values.append([
                jnp.sum(jnp.where(mask, found[c * rows:(c + 1) * rows], 0.0), axis=0, keepdims=True)
                for c in range(3)
            ])
            hots.append(hot)
            masks.append(mask)
        traction = [factor * (values[0][c] - values[1][c]) for c in range(3)]
        high = [t.astype(BF16).astype(F32) for t in traction]
        parts = high + [t - h for t, h in zip(traction, high)]
        for hot, mask, acc in zip(hots, masks, (acc_f, acc_n)):
            spread = jnp.concatenate([jnp.where(mask, t, 0.0).astype(BF16) for t in parts], axis=0)
            out = lax.dot_general(spread, hot, (((1,), (1,)), ((), ())), preferred_element_type=F32)
            acc[...] += out[:size] + out[size:]

    if sources <= 16:
        for q in range(sources // 2):
            chunk(q)
    else:
        pl.loop(0, sources // 2)(chunk)

    for c in range(3):
        force = acc_f[c * rows:(c + 1) * rows]
        bx = half.shape[1]
        fluid[c, :, :hy] = half[c, :, :hy] - force[:, :bz].reshape(bx, hy, bz)
        fluid[c, :, hy:] = half[c, :, hy:] - force[:, bz:].reshape(bx, hy, bz)
    fluid[3] = half[3]
    for p, z, c, r, l in pieces():
        terms[p, z, c] = acc_n[r, l]


def piece_split(nx, tail):
    lp = min(2, nx)
    return nx // lp, lp, tail[0], tail[1]


def on_device(sizes, fluid_state, shell_disp, quad_weights, quad_elements, owner_cells, owner_counts):
    nx, ny, nz = sizes
    plane = nx * ny
    slots = quad_weights.shape[2]
    ranks = quad_weights.shape[1]
    block = fluid_state.shape
    nodes_here = shell_disp.shape[1]
    lanes = 2 * block[3]
    lp = min(2, nx)
    rp = nx // lp
    pr, pw = nodes_here // lanes // rp, lanes // lp
    piece = (3, pr, pw)
    shell = shell_disp.reshape(3, rp, pr, lp, pw).transpose(1, 3, 0, 2, 4).reshape((nx,) + piece)
    rec = jnp.concatenate([quad_weights[0], quad_elements[0].astype(F32)], axis=1)
    rec = rec.reshape(plane, nz, 1, 2 * slots).transpose(1, 0, 2, 3)
    live = (jnp.arange(slots, dtype=jnp.int32)[None, :] < owner_counts[0][:, None]).astype(F32)
    halves = ranks // 2
    live = jnp.concatenate([live[:halves], live[halves:]], axis=1)
    cells = jnp.concatenate([owner_cells[0][:halves], owner_cells[0][halves:]], axis=1)

    vmem = pl.BlockSpec(memory_space=pltpu.VMEM)
    shape = lambda s: jax.ShapeDtypeStruct(s, F32)
    line = (nz,) + piece
    full = (plane,) + line
    sem = lambda n: pltpu.SemaphoreType.DMA((2, max(n, 1)))
    params = lambda i: pltpu.CompilerParams(collective_id=i, has_side_effects=True, vmem_limit_bytes=40 << 20)

    half, nodes, records = pl.pallas_call(
        functools.partial(first_kernel, sizes),
        out_shape=(shape(block), shape(full), shape((plane, nz, 1, 2 * slots))),
        in_specs=[vmem] * 3, out_specs=(vmem,) * 3,
        scratch_shapes=[
            pltpu.VMEM(line, F32), pltpu.VMEM((nz, plane, 1, 2 * slots), F32),
            sem(nz - 1), sem(plane - 1), sem(nz - 1), sem(plane - 1),
        ] + sweep_scratch(block),
        compiler_params=params(0),
    )(fluid_state, shell, rec)
    weights_ids = records.reshape(ranks, 2 * slots)

    rows = ny * nz * rp * pr
    couple = pl.pallas_call(
        functools.partial(couple_kernel, sizes),
        out_shape=(shape(block), shape(full)),
        in_specs=[vmem] * 5, out_specs=(vmem,) * 2,
        scratch_shapes=[
            pltpu.VMEM((6 * rows, lanes), BF16), pltpu.VMEM((6 * rows, lanes), BF16),
            pltpu.VMEM((3 * rows, lanes), F32), pltpu.VMEM((3 * rows, lanes), F32),
            pltpu.VMEM((3 * rows, lanes), F32),
        ],
        compiler_params=pltpu.CompilerParams(vmem_limit_bytes=40 << 20),
    )
    fluid, terms = couple(half, nodes, weights_ids, cells, live)

    reduce_scratch = [pltpu.VMEM((plane - 1,) + line, F32), pltpu.VMEM(line, F32), pltpu.VMEM((nz - 1,) + piece, F32)]
    half, nodes, mine = pl.pallas_call(
        functools.partial(middle_kernel, sizes),
        out_shape=(shape(block), shape(full), shape(piece)),
        in_specs=[vmem] * 3, out_specs=(vmem,) * 3,
        scratch_shapes=reduce_scratch + [
            pltpu.VMEM(line, F32), sem(plane - 1), sem(nz - 1), sem(nz - 1), sem(plane - 1),
        ] + sweep_scratch(block),
        compiler_params=params(1),
    )(fluid, shell, terms)
    fluid, terms = couple(half, nodes, weights_ids, cells, live)

    out = pl.pallas_call(
        functools.partial(last_kernel, sizes),
        out_shape=shape((nx,) + piece),
        in_specs=[vmem] * 2, out_specs=vmem,
        scratch_shapes=reduce_scratch + [pltpu.VMEM(piece, F32), sem(plane - 1), sem(nz - 1), sem(nx - 1)],
        compiler_params=params(2),
    )(mine, terms)
    out = out.reshape(rp, lp, 3, pr, pw).transpose(2, 0, 3, 1, 4).reshape(3, nodes_here)
    return fluid, out


def solution(mesh):
    sizes = tuple(mesh.shape[a] for a in AXES)
    return jax.shard_map(
        functools.partial(on_device, sizes),
        mesh=mesh,
        in_specs=(
            P(None, "gx", "gy", "gz"),
            P(None, ("gy", "gz")),
            P(("gx", "gy", "gz"), None, None),
            P(("gx", "gy", "gz"), None, None),
            P(("gx", "gy", "gz"), None, None),
            P(("gx", "gy", "gz"), None),
        ),
        out_specs=(P(None, "gx", "gy", "gz"), P(None, ("gy", "gz"))),
        check_vma=False,
    )
```

time: 1420 us -> 70.9 us (0.05)
  blocking collectives: 770 us -> 0 us
  waiting for transfers between devices: 316 us -> 0 us
  local copies, waits for them, and re-layouts: 151 us -> 4.36 us
  other arithmetic: 107 us -> 0.33 us
  Pallas kernels: 0 us -> 65.1 us
  starting transfers between devices: 55 us -> 0 us
  between operations: 15.5 us -> 0.74 us
    all_gather x2 -> x0, blocking collectives: 713 us -> none  [on_device(): all_nodes = lax.all_gather(shell_disp, ('gy', 'gz'), axis=1, tiled=True)]
    reduce_scatter x2 -> x0, waiting for transfers between devices: 309 us -> none  [on_device(): lax.psum_scatter(node_terms, ('gy', 'gz'), scatter_dimension=1, tiled=True)]
    scatter-add x4 -> x0, other arithmetic: 77.2 us -> none  [the longest x2 40.2 us: on_device(): forcing = jnp.zeros_like(flat_vel).at[:, cells_local].add(traction)]
    pallas_call x0 -> x5, Pallas kernels: none -> 65.1 us  [the longest x1 23.7 us: on_device(): pl.pallas_call(functools.partial(middle_kernel, sizes), out_shape=(shape(...]
    psum x2 -> x0, blocking collectives: 56.9 us -> none  [on_device(): node_loads = lax.psum(partial_loads, 'gx')]
    gather x8 -> x0, local copies, waits for them, and re-layouts: 49.8 us -> none  [the longest x4 26.5 us: on_device(): velocity = flat_vel[:, cells_local]]
    ppermute x12 -> x0, starting transfers between devices: 28.4 us -> none  [the longest x6 20.3 us: with_halo(): lax.ppermute(tail, axis, [(i, (i + 1) % count) for i in range(ends)])]
    all_to_all x4 -> x0, starting transfers between devices: 26.5 us -> none  [the longest x2 16 us: on_device(): lax.all_to_all(traction, ('gx', 'gy', 'gz'), split_axis=1, concat_axis=1,...]
  transfers between devices with their start and end apart: 18 -> 0, of which waited for: 3 -> 0; matrix products, arithmetic and copies ran while one was open for 9% -> 0% of each run, Pallas kernels for 0% -> 0%
where the time goes in v1:
time: 70.9 us; the launch traced here: 70.5 us
  Pallas kernels  65.1 us (92%)
  local copies, waits for them, and re-layouts  4.36 us (6%)
  between operations  0.74 us (1%)
    pallas_call x1, Pallas kernels, on_device(): pl.pallas_call(functools.partial(middle_kernel, sizes), out_shape=(shape(...  23.7 us
    pallas_call x1, Pallas kernels, on_device(): pl.pallas_call(functools.partial(first_kernel, sizes), out_shape=(shape(b...  17.1 us
    pallas_call x1, Pallas kernels, on_device(): pl.pallas_call(functools.partial(last_kernel, sizes), out_shape=shape((nx...  14.2 us
    pallas_call x2, Pallas kernels, on_device(): fluid, terms = couple(half, nodes, weights_ids, cells, live)  10 us
    unnamed x10, local copies, waits for them, and re-layouts  2.9 us

profile of v1, /device:TPU:0, one launch (start us, length us, event | category | flops | bytes accessed | tf_op | source)
XLA Modules:
  0.0 70.5 jit_solution(12395550526460006697)
XLA Ops:
  0.6 0.0 copy-start.2
  0.6 0.7 %copy.9 = f32[8,4,1,64]{3,2,0,1:T(1,128)S(1)} copy(f32[8,4,1,64]{3,1,0,2:T(4,128)} %bitcast.26) | data formatting | bytes 16384 | tf_op jit(solution)/shard_map/concatenate | solution.py:440
  1.4 0.0 copy-done.2
  1.4 0.0 copy-start.4
  1.4 0.1 maximum_bitcast_fusion.rec
  1.6 0.5 copy-done.4
  2.1 0.1 fusion
  2.2 0.0 copy-start.3
  2.2 0.1 pad_maximum_fusion.live
  2.2 0.6 copy-done.3
  2.9 0.0 copy-start.1
  2.9 0.1 pad_add_fusion.cells
  3.0 0.7 copy-done.1
  3.7 0.0 copy-start
  3.7 1.0 %copy-done = f32[4,16,16,128]{3,2,1,0:T(8,128)S(1)} copy-done((f32[4,16,16,128]{3,2,1,0:T(8,128)S(1)}, f32[4,16,16,128]{3,2,1,0:T(8,128)}, u32[]{:S(2)}) %copy-start) | copy-done | bytes 524312
  4.7 17.1 %shard_map.77 = (f32[4,16,16,128]{3,2,1,0:T(8,128)S(1)}, f32[8,4,3,8,128]{4,3,2,1,0:T(8,128)S(1)}, f32[8,4,1,128]{3,2,1,0:T(1,128)S(1)}) custom-call(f32[4,16,16,128]{3,2,1,0:T(8,128)S(1)} %copy-done, f32[2,3,8,128]{3,2,1,0:T(8,128)S(1)} %bitcast.20, f32[4,8,1,128]{3,2,1,0:T(1,128)S(1)} %maximum_bitcast_fusion.rec), custom_call_target="tpu_custom_call" | custom-call | tf_op jit(solution)/shard_map/pallas_call | solution.py:454
  21.9 4.6 %shard_map.78 = (f32[4,16,16,128]{3,2,1,0:T(8,128)S(1)}, f32[8,4,3,8,128]{4,3,2,1,0:T(8,128)S(1)}) custom-call(f32[4,16,16,128]{3,2,1,0:T(8,128)S(1)} %get-tuple-element.12.half, f32[8,4,3,8,128]{4,3,2,1,0:T(8,128)S(1)} %get-tuple-element.13.nodes, f32[32,128]{1,0:T(8,128)S(1)} %bitcast.23, s32[16,128]{1,0:T(8,128)S(1)} %pad_add_fusion.cells, ...), custom_call_target="tpu_custom_call" | custom-call | tf_op jit(solution)/shard_map/pallas_call | solution.py:478
  26.5 23.7 %shard_map.79 = (f32[4,16,16,128]{3,2,1,0:T(8,128)S(1)}, f32[8,4,3,8,128]{4,3,2,1,0:T(8,128)S(1)}, f32[3,8,128]{2,1,0:T(8,128)S(1)}) custom-call(f32[4,16,16,128]{3,2,1,0:T(8,128)S(1)} %get-tuple-element.15.f, f32[2,3,8,128]{3,2,1,0:T(8,128)S(1)} %bitcast.21, f32[8,4,3,8,128]{4,3,2,1,0:T(8,128)S(1)} %get-tuple-element.16.terms), custom_call_target="tpu_custom_call" | custom-call | tf_op jit(solution)/shard_map/pallas_call | solution.py:481
  50.2 5.4 %shard_map.80 = (f32[4,16,16,128]{3,2,1,0:T(8,128)}, f32[8,4,3,8,128]{4,3,2,1,0:T(8,128)S(1)}) custom-call(f32[4,16,16,128]{3,2,1,0:T(8,128)S(1)} %get-tuple-element.17.half, f32[8,4,3,8,128]{4,3,2,1,0:T(8,128)S(1)} %get-tuple-element.18.nodes, f32[32,128]{1,0:T(8,128)S(1)} %bitcast.24, s32[16,128]{1,0:T(8,128)S(1)} %pad_add_fusion.cells, ...), custom_call_target="tpu_custom_call" | custom-call | tf_op jit(solution)/shard_map/pallas_call | solution.py:490
  55.6 14.2 %shard_map.81 = f32[2,3,8,128]{3,2,1,0:T(8,128)S(1)} custom-call(f32[3,8,128]{2,1,0:T(8,128)S(1)} %get-tuple-element.20.shell, f32[8,4,3,8,128]{4,3,2,1,0:T(8,128)S(1)} %get-tuple-element.21.terms), custom_call_target="tpu_custom_call" | custom-call | tf_op jit(solution)/shard_map/pallas_call | solution.py:492
  69.9 0.6 reshape.41
  (7 shorter events, 0.1 us)
Async XLA Ops:
  0.6 0.8 %copy-start.2 = (s32[1,32,64]{2,1,0:T(8,128)S(1)}, s32[1,32,64]{2,1,0:T(8,128)}, u32[]{:S(2)}) copy-start(s32[1,32,64]{2,1,0:T(8,128)} %param.9) | copy-start | bytes 24580
  1.4 0.7 copy-start.4
  2.2 0.7 %copy-start.3 = (s32[1,32,64]{2,1,0:T(8,128)S(1)}, s32[1,32,64]{2,1,0:T(8,128)}, u32[]{:S(2)}) copy-start(s32[1,32,64]{2,1,0:T(8,128)} %param.10) | copy-start | bytes 24580
  2.9 0.8 %copy-start.1 = (f32[3,2048]{1,0:T(4,128)S(1)}, f32[3,2048]{1,0:T(4,128)}, u32[]{:S(2)}) copy-start(f32[3,2048]{1,0:T(4,128)} %param.7) | copy-start | bytes 73732
  3.7 1.0 %copy-start = (f32[4,16,16,128]{3,2,1,0:T(8,128)S(1)}, f32[4,16,16,128]{3,2,1,0:T(8,128)}, u32[]{:S(2)}) copy-start(f32[4,16,16,128]{3,2,1,0:T(8,128)} %f.1) | copy-start | bytes 1572868

commit v2 on v1

v2 whole, which is shorter than its diff:
```python
import functools

import jax
import jax.numpy as jnp
from jax import lax
from jax.experimental import pallas as pl
from jax.experimental.pallas import tpu as pltpu
from jax.sharding import PartitionSpec as P

ITERS = 2

advection = 0.2
penalty = 0.5
relaxation = 0.05
AXES = ("gx", "gy", "gz")
MESH = pl.DeviceIdType.MESH
F32 = jnp.float32
BF16 = jnp.bfloat16


class Place:
    def __init__(self, sizes):
        self.nx, self.ny, self.nz = sizes
        self.plane = self.nx * self.ny
        self.x, self.y, self.z = (lax.axis_index(a) for a in AXES)
        self.p = self.x * self.ny + self.y

    def plane_peer(self, d):
        p = lax.rem(self.p + d, self.plane)
        return p, (lax.div(p, self.ny), lax.rem(p, self.ny), self.z)

    def line_peer(self, d):
        z = lax.rem(self.z + d, self.nz)
        return z, (self.x, self.y, z)

    def barrier(self):
        sem = pltpu.get_barrier_semaphore()
        for d in range(1, self.plane):
            pl.semaphore_signal(sem, inc=1, device_id=self.plane_peer(d)[1], device_id_type=MESH)
        for d in range(1, self.nz):
            pl.semaphore_signal(sem, inc=1, device_id=self.line_peer(d)[1], device_id_type=MESH)
        pl.semaphore_wait(sem, self.plane - 1 + self.nz - 1)


def send(src, dst, sems, k, device):
    return pltpu.make_async_remote_copy(
        src_ref=src, dst_ref=dst, send_sem=sems.at[0, k], recv_sem=sems.at[1, k],
        device_id=device, device_id_type=MESH,
    )


def start_all(copies):
    for c in copies:
        c.start()
    return copies


def wait_all(copies):
    for c in copies:
        c.wait()


class Halo:
    def __init__(self, here, count, device_of, srcs, dsts, sems):
        self.has = (here > 0, here < count - 1)
        self.copies = []
        for s in (0, 1):
            there = jnp.clip(here + (2 * s - 1), 0, count - 1)
            self.copies.append(send(srcs[s], dsts[1 - s], sems, s, device_of(there)))

    def start(self):
        for s in (0, 1):
            @pl.when(self.has[s])
            def _():
                self.copies[s].start()

    def wait(self):
        for s in (0, 1):
            @pl.when(self.has[s])
            def _():
                self.copies[s].wait_send()
                self.copies[1 - s].wait_recv()


class Sweep:
    def __init__(self, at, half, fx, sx, sxy, ys, yh, zs, zh, sem_x, sem_y, sem_z):
        self.at, self.half, self.fx, self.sx, self.sxy = at, half, fx, sx, sxy
        self.ys, self.yh, self.zs, self.zh = ys, yh, zs, zh
        self.nf, self.bx, self.by, self.bz = half.shape
        bx = self.bx
        self.hx = Halo(at.x, at.nx, lambda x: (x, at.y, at.z),
                       (fx.at[:, 1], fx.at[:, bx]), (fx.at[:, 0], fx.at[:, bx + 1]), sem_x)
        self.hy = Halo(at.y, at.ny, lambda y: (at.x, y, at.z),
                       (ys.at[0], ys.at[1]), (yh.at[0], yh.at[1]), sem_y)
        self.hz = Halo(at.z, at.nz, lambda z: (at.x, at.y, z),
                       (zs.at[0], zs.at[1]), (zh.at[0], zh.at[1]), sem_z)

    def clear_ends(self):
        for s, edge in ((0, 0), (1, self.bx + 1)):
            @pl.when(jnp.logical_not(self.hx.has[s]))
            def _():
                self.fx[:, edge] = jnp.zeros((self.nf, self.by, self.bz), F32)

            @pl.when(jnp.logical_not(self.hy.has[s]))
            def _():
                self.yh[s] = jnp.zeros(self.yh.shape[1:], F32)

            @pl.when(jnp.logical_not(self.hz.has[s]))
            def _():
                self.zh[s] = jnp.zeros(self.zh.shape[1:], F32)

    def start_x(self):
        self.hx.start()

    def x_then_start_y(self):
        self.hx.wait()

        def step(x, _):
            for c in range(self.nf):
                mid = self.fx[c, x + 1]
                s = 0.25 * self.fx[c, x] + 0.5 * mid + 0.25 * self.fx[c, x + 2]
                self.sx[c, x] = s
                row = c * self.bx + x
                self.ys[0, 0, pl.ds(row, 1), :] = mid[0:1]
                self.ys[1, 0, pl.ds(row, 1), :] = mid[self.by - 1:]
                self.ys[0, 1, pl.ds(row, 1), :] = s[0:1]
                self.ys[1, 1, pl.ds(row, 1), :] = s[self.by - 1:]
            return 0

        lax.fori_loop(0, self.bx, step, 0)
        self.hy.start()

    def shift_y(self, tile, c, x, kind):
        sub = lax.broadcasted_iota(jnp.int32, tile.shape, 0)
        row = c * self.bx + x
        lower = jnp.where(sub == 0, self.yh[0, kind, pl.ds(row, 1), :], pltpu.roll(tile, 1, axis=0))
        upper = jnp.where(sub == self.by - 1, self.yh[1, kind, pl.ds(row, 1), :],
                          pltpu.roll(tile, self.by - 1, axis=0))
        return lower, upper

    def y_then_start_z(self):
        self.hy.wait()
        lane = lax.broadcasted_iota(jnp.int32, (self.by, self.zs.shape[2]), 1)
        group = self.nf * self.bx

        def step(x, faces):
            low, high = faces
            for c in range(self.nf):
                tile = self.sx[c, x]
                lower, upper = self.shift_y(tile, c, x, 1)
                s = 0.25 * lower + 0.5 * tile + 0.25 * upper
                self.sxy[c, x] = s
                raw = self.fx[c, x + 1]
                k = c * self.bx + x
                low = jnp.where(lane == k, raw[:, 0:1], low)
                low = jnp.where(lane == k + group, s[:, 0:1], low)
                high = jnp.where(lane == k, raw[:, self.bz - 1:], high)
                high = jnp.where(lane == k + group, s[:, self.bz - 1:], high)
            return low, high

        zero = jnp.zeros(lane.shape, F32)
        low, high = lax.fori_loop(0, self.bx, step, (zero, zero))
        self.zs[0] = low
        self.zs[1] = high
        self.hz.start()

    def finish(self):
        self.hz.wait()
        lane = lax.broadcasted_iota(jnp.int32, (self.by, self.bz), 1)
        width = self.zs.shape[2]
        group = self.nf * self.bx

        def step(x, _):
            turn = lax.rem(width - x, width)
            low, high = (pltpu.roll(self.zh[s], turn, axis=1) for s in (0, 1))

            def shift_z(tile, k):
                lower = jnp.where(lane == 0, low[:, k:k + 1], pltpu.roll(tile, 1, axis=1))
                upper = jnp.where(lane == self.bz - 1, high[:, k:k + 1], pltpu.roll(tile, self.bz - 1, axis=1))
                return lower, upper

            u = [self.fx[c, x + 1] for c in range(3)]
            for c in range(self.nf):
                raw = self.fx[c, x + 1]
                s = self.sxy[c, x]
                lower, upper = shift_z(s, group + c * self.bx)
                smoothed = 0.25 * lower + 0.5 * s + 0.25 * upper
                grad_x = 0.5 * (self.fx[c, x + 2] - self.fx[c, x])
                lower, upper = self.shift_y(raw, c, x, 0)
                grad_y = 0.5 * (upper - lower)
                lower, upper = shift_z(raw, c * self.bx)
                grad_z = 0.5 * (upper - lower)
                self.half[c, x] = smoothed - advection * (u[0] * grad_x + u[1] * grad_y + u[2] * grad_z)
                if c == 3:
                    for v, g in enumerate((grad_x, grad_y, grad_z)):
                        self.half[v, x] = self.half[v, x] - advection * g
            return 0

        lax.fori_loop(0, self.bx, step, 0)


def sweep_scratch(block):
    nf, bx, by, bz = block
    width = -(-2 * nf * bx // 128) * 128
    dma = pltpu.SemaphoreType.DMA((2, 2))
    return [
        pltpu.VMEM((nf, bx + 2, by, bz), F32), pltpu.VMEM(block, F32), pltpu.VMEM(block, F32),
        pltpu.VMEM((2, 2, nf * bx, bz), F32), pltpu.VMEM((2, 2, nf * bx, bz), F32),
        pltpu.VMEM((2, by, width), F32), pltpu.VMEM((2, by, width), F32), dma, dma, dma,
    ]


def gather_line(at, piece, line, sems):
    return start_all([send(piece, line.at[at.z], sems, d - 1, at.line_peer(d)[1]) for d in range(1, at.nz)])


def gather_plane(at, line, nodes, sems):
    return start_all([send(line, nodes.at[at.p], sems, d - 1, at.plane_peer(d)[1]) for d in range(1, at.plane)])


def reduce_plane(at, terms, landed, sems):
    copies = []
    for d in range(1, at.plane):
        p, device = at.plane_peer(d)
        copies.append(send(terms.at[p], landed.at[d - 1], sems, d - 1, device))
    return start_all(copies)


def sum_plane(at, terms, landed, sums):
    total = terms[at.p]
    for d in range(1, at.plane):
        total = total + landed[d - 1]
    sums[...] = total


def reduce_line(at, sums, landed, sems):
    copies = []
    for d in range(1, at.nz):
        z, device = at.line_peer(d)
        copies.append(send(sums.at[z], landed.at[d - 1], sems, d - 1, device))
    return start_all(copies)


def sum_line(at, sums, landed):
    total = sums[at.z]
    for d in range(1, at.nz):
        total = total + landed[d - 1]
    return total


class Couple:
    def __init__(self, sizes, half, nodes, terms, weights_ids, cells, hs, ns, nf32, acc_f, acc_n, speed):
        self.sizes = sizes
        self.half, self.nodes, self.terms = half, nodes, terms
        self.weights_ids, self.cells = weights_ids, cells
        self.hs, self.ns, self.nf32, self.acc_f, self.acc_n, self.speed = hs, ns, nf32, acc_f, acc_n, speed
        self.rows, self.lanes = acc_f.shape[0] // 3, acc_f.shape[1]
        self.size = 3 * self.rows
        self.sources, self.width = cells.shape
        _, self.bx, self.by, self.bz = half.shape
        self.hy = self.by // 2

    def chunks(self, step):
        if self.sources <= 16:
            for q in range(self.sources // 2):
                step(q)
        else:
            pl.loop(0, self.sources // 2)(step)

    def split_store(self, ref, c, value):
        hi = value.astype(BF16)
        ref[c * self.rows:(c + 1) * self.rows] = hi
        ref[self.size + c * self.rows:self.size + (c + 1) * self.rows] = (value - hi.astype(F32)).astype(BF16)

    def pieces(self):
        nx, ny, nz = self.sizes
        pr, pw = self.nodes.shape[3:]
        lp = min(2, nx)
        rp = nx // lp
        for g in range(nx):
            r0, l0 = (g // lp) * pr, (g % lp) * pw
            for y in range(ny):
                for z in range(nz):
                    for c in range(3):
                        r = c * self.rows + (y * nz + z) * (rp * pr) + r0
                        yield g * ny + y, z, c, slice(r, r + pr), slice(l0, l0 + pw)

    def both(self, read, q):
        return jnp.concatenate([read(2 * q), read(2 * q + 1)], axis=1)

    def cell(self, q):
        return self.both(lambda i: self.cells[pl.ds(i, 1), :], q)

    def pair(self, i):
        return self.weights_ids[i], self.weights_ids[i + self.sources]

    def left(self):
        return lax.broadcasted_iota(jnp.int32, (1, self.width), 1) < self.width // 2

    def weight(self, i):
        top, bottom = self.pair(i)
        return jnp.where(self.left(), top, pltpu.roll(bottom, self.width // 2, axis=1))

    def ident(self, i):
        top, bottom = self.pair(i)
        return jnp.where(self.left(), pltpu.roll(top, self.width // 2, axis=1), bottom)

    def cell_place(self, q):
        cell = self.cell(q)
        y = lax.rem(lax.div(cell, self.bz), self.by)
        x = lax.div(cell, self.by * self.bz)
        return self.hots(x * self.hy + lax.rem(y, self.hy), lax.div(y, self.hy) * self.bz + lax.rem(cell, self.bz))

    def node_place(self, q):
        node = self.both(self.ident, q).astype(jnp.int32)
        return self.hots(lax.div(node, self.lanes), lax.rem(node, self.lanes))

    def hots(self, row, lane):
        lane_of = lax.broadcasted_iota(jnp.int32, (self.lanes, 2 * self.width), 0)
        row_of = lax.broadcasted_iota(jnp.int32, (self.rows, 2 * self.width), 0)
        return jnp.where(lane_of == lane, 1.0, 0.0).astype(BF16), row_of == row

    def find(self, ref, hot, mask):
        found = jnp.dot(ref[...], hot, preferred_element_type=F32)
        found = found[:self.size] + found[self.size:]
        return [
            jnp.sum(jnp.where(mask, found[c * self.rows:(c + 1) * self.rows], 0.0), axis=0, keepdims=True)
            for c in range(3)
        ]

    def spread(self, hot, mask, traction, acc):
        high = [t.astype(BF16).astype(F32) for t in traction]
        parts = high + [t - h for t, h in zip(traction, high)]
        values = jnp.concatenate([jnp.where(mask, t, 0.0).astype(BF16) for t in parts], axis=0)
        out = lax.dot_general(values, hot, (((1,), (1,)), ((), ())), preferred_element_type=F32)
        acc[...] += out[:self.size] + out[self.size:]

    def gather_cells(self):
        for c in range(3):
            value = self.half[c]
            top = value[:, :self.hy].reshape(self.rows, self.bz)
            low = value[:, self.hy:].reshape(self.rows, self.bz)
            self.split_store(self.hs, c, jnp.concatenate([top, low], axis=1))
        self.acc_f[...] = jnp.zeros_like(self.acc_f)
        self.acc_n[...] = jnp.zeros_like(self.acc_n)

        def step(q):
            for c, v in enumerate(self.find(self.hs, *self.cell_place(q))):
                self.speed[q, c:c + 1] = v

        self.chunks(step)

    def nodes_to_terms(self):
        for p, z, c, r, l in self.pieces():
            self.nf32[r, l] = self.nodes[p, z, c]
        for c in range(3):
            self.split_store(self.ns, c, self.nf32[c * self.rows:(c + 1) * self.rows])
        total = self.bx * self.by * self.bz

        def step(q):
            factor = jnp.where(self.cell(q) < total, penalty * self.both(self.weight, q), 0.0)
            hot, mask = self.node_place(q)
            shell = self.find(self.ns, hot, mask)
            traction = [factor * (self.speed[q, c:c + 1] - shell[c]) for c in range(3)]
            for c in range(3):
                self.speed[q, c:c + 1] = traction[c]
            self.spread(hot, mask, traction, self.acc_n)

        self.chunks(step)
        for p, z, c, r, l in self.pieces():
            self.terms[p, z, c] = self.acc_n[r, l]

    def force_cells(self, fluid, first):
        def step(q):
            hot, mask = self.cell_place(q)
            self.spread(hot, mask, [self.speed[q, c:c + 1] for c in range(3)], self.acc_f)

        self.chunks(step)
        bx, hy, bz = self.bx, self.hy, self.bz
        for c in range(3):
            force = self.acc_f[c * self.rows:(c + 1) * self.rows]
            fluid[c, first:first + bx, :hy] = self.half[c, :, :hy] - force[:, :bz].reshape(bx, hy, bz)
            fluid[c, first:first + bx, hy:] = self.half[c, :, hy:] - force[:, bz:].reshape(bx, hy, bz)
        fluid[3, first:first + bx] = self.half[3]


def whole_kernel(sizes, fluid_in, shell_in, rec_in, cells_in, fluid, out, *refs):
    refs = list(refs)
    take = lambda n: [refs.pop(0) for _ in range(n)]
    shell, rec, cells, sem_in = take(4)
    line0, line1, nodes0, nodes1, rec_line, records = take(6)
    halves, terms = take(2), take(2)
    reduce0, reduce1 = take(3), take(3)
    mine, last = take(2)
    sem_nl0, sem_np0, sem_rl, sem_rp = take(4)
    sem_ap0, sem_al0, sem_nl1, sem_np1, sem_ap1, sem_al1, sem_g = take(7)
    couple_refs = take(6)
    sweep_refs = take(10), take(10)
    at = Place(sizes)
    sweeps = [Sweep(at, h, *r) for h, r in zip(halves, sweep_refs)]
    bx = halves[0].shape[1]
    fetches = [
        pltpu.make_async_copy(src, dst, sem_in.at[i])
        for i, (src, dst) in enumerate((
            (fluid_in, sweep_refs[0][0].at[:, 1:bx + 1]), (shell_in, shell), (rec_in, rec), (cells_in, cells)))
    ]
    start_all(fetches)
    for sweep in sweeps:
        sweep.clear_ends()
    at.barrier()
    wait_all(fetches)
    first, second = sweeps
    couples = [Couple(sizes, halves[i], (nodes0, nodes1)[i], terms[i], RecordRows(records), cells, *couple_refs)
               for i in (0, 1)]

    first.start_x()
    node_copies = gather_line(at, shell.at[at.x], line0, sem_nl0)
    rec_copies = []
    for d in range(1, at.nz):
        z, device = at.line_peer(d)
        rec_copies.append(send(rec.at[:, z], rec_line.at[at.z], sem_rl, d - 1, device))
    start_all(rec_copies)
    line0[at.z] = shell[at.x]
    rec_line[at.z] = rec[:, at.z]
    first.x_then_start_y()
    wait_all(node_copies)
    node_copies = gather_plane(at, line0, nodes0, sem_np0)
    wait_all(rec_copies)
    rec_copies = []
    for d in range(1, at.plane):
        p, device = at.plane_peer(d)
        rec_copies.append(send(rec_line.at[:, p], records.at[at.p], sem_rp, d - 1, device))
    start_all(rec_copies)
    nodes0[at.p] = line0[...]
    records[at.p] = rec_line[:, at.p]
    first.y_then_start_z()
    first.finish()
    couples[0].gather_cells()
    wait_all(node_copies)
    wait_all(rec_copies)
    couples[0].nodes_to_terms()

    landed_p, sums, landed_l = reduce0
    copies = reduce_plane(at, terms[0], landed_p, sem_ap0)
    couples[0].force_cells(second.fx, 1)
    second.start_x()
    second.x_then_start_y()
    wait_all(copies)
    sum_plane(at, terms[0], landed_p, sums)
    copies = reduce_line(at, sums, landed_l, sem_al0)
    second.y_then_start_z()
    wait_all(copies)
    fresh = shell[at.x] + relaxation * sum_line(at, sums, landed_l)
    mine[...] = fresh
    line1[at.z] = fresh
    copies = gather_line(at, mine, line1, sem_nl1)
    second.finish()
    wait_all(copies)
    copies = gather_plane(at, line1, nodes1, sem_np1)
    nodes1[at.p] = line1[...]
    couples[1].gather_cells()
    wait_all(copies)
    couples[1].nodes_to_terms()

    landed_p, sums, landed_l = reduce1
    copies = reduce_plane(at, terms[1], landed_p, sem_ap1)
    couples[1].force_cells(fluid, 0)
    wait_all(copies)
    sum_plane(at, terms[1], landed_p, sums)
    copies = reduce_line(at, sums, landed_l, sem_al1)
    wait_all(copies)
    fresh = mine[...] + relaxation * sum_line(at, sums, landed_l)
    last[...] = fresh
    copies = []
    for d in range(1, at.nx):
        x = lax.rem(at.x + d, at.nx)
        copies.append(send(last, out.at[at.x], sem_g, d - 1, (x, at.y, at.z)))
    start_all(copies)
    out[at.x] = fresh
    wait_all(copies)


class RecordRows:
    def __init__(self, records):
        self.records, self.nz = records, records.shape[1]

    def __getitem__(self, i):
        if isinstance(i, int):
            return self.records[i // self.nz, i % self.nz]
        return self.records[lax.div(i, self.nz), lax.rem(i, self.nz)]


def on_device(sizes, fluid_state, shell_disp, quad_weights, quad_elements, owner_cells, owner_counts):
    nx, ny, nz = sizes
    plane = nx * ny
    slots = quad_weights.shape[2]
    ranks = quad_weights.shape[1]
    block = fluid_state.shape
    nodes_here = shell_disp.shape[1]
    lanes = 2 * block[3]
    lp = min(2, nx)
    rp = nx // lp
    pr, pw = nodes_here // lanes // rp, lanes // lp
    piece = (3, pr, pw)
    shell = shell_disp.reshape(3, rp, pr, lp, pw).transpose(1, 3, 0, 2, 4).reshape((nx,) + piece)
    rec = jnp.concatenate([quad_weights[0], quad_elements[0].astype(F32)], axis=1)
    rec = rec.reshape(plane, nz, 1, 2 * slots)
    live = jnp.arange(slots, dtype=jnp.int32)[None, :] < owner_counts[0][:, None]
    cells = jnp.where(live, owner_cells[0], block[1] * block[2] * block[3])
    halves = ranks // 2
    cells = jnp.concatenate([cells[:halves], cells[halves:]], axis=1)

    shape = lambda s: jax.ShapeDtypeStruct(s, F32)
    buf = lambda s: pltpu.VMEM(s, F32)
    line = (nz,) + piece
    full = (plane,) + line
    sem = lambda n: pltpu.SemaphoreType.DMA((2, max(n, 1)))
    reduce_scratch = [buf((plane - 1,) + line), buf(line), buf((nz - 1,) + piece)]
    rows = ny * nz * rp * pr
    scratch = [
        buf(shell.shape), buf(rec.shape), pltpu.VMEM(cells.shape, jnp.int32), pltpu.SemaphoreType.DMA((4,)),
        buf(line), buf(line), buf(full), buf(full), buf((nz, plane, 1, 2 * slots)), buf((plane, nz, 1, 2 * slots)),
        buf(block), buf(block), buf(full), buf(full),
        *reduce_scratch, *reduce_scratch, buf(piece), buf(piece),
        sem(nz - 1), sem(plane - 1), sem(nz - 1), sem(plane - 1),
        sem(plane - 1), sem(nz - 1), sem(nz - 1), sem(plane - 1), sem(plane - 1), sem(nz - 1), sem(nx - 1),
        pltpu.VMEM((6 * rows, lanes), BF16), pltpu.VMEM((6 * rows, lanes), BF16),
        buf((3 * rows, lanes)), buf((3 * rows, lanes)), buf((3 * rows, lanes)), buf((ranks // 4, 3, 4 * slots)),
        *sweep_scratch(block), *sweep_scratch(block),
    ]
    anywhere, vmem = pl.BlockSpec(memory_space=pl.ANY), pl.BlockSpec(memory_space=pltpu.VMEM)
    fluid, out = pl.pallas_call(
        functools.partial(whole_kernel, sizes),
        out_shape=(shape(block), shape((nx,) + piece)),
        in_specs=[anywhere] * 4, out_specs=(vmem, vmem),
        scratch_shapes=scratch,
        compiler_params=pltpu.CompilerParams(collective_id=0, has_side_effects=True, vmem_limit_bytes=56 << 20),
    )(fluid_state, shell, rec, cells)
    out = out.reshape(rp, lp, 3, pr, pw).transpose(2, 0, 3, 1, 4).reshape(3, nodes_here)
    return fluid, out


def solution(mesh):
    sizes = tuple(mesh.shape[a] for a in AXES)
    return jax.shard_map(
        functools.partial(on_device, sizes),
        mesh=mesh,
        in_specs=(
            P(None, "gx", "gy", "gz"),
            P(None, ("gy", "gz")),
            P(("gx", "gy", "gz"), None, None),
            P(("gx", "gy", "gz"), None, None),
            P(("gx", "gy", "gz"), None, None),
            P(("gx", "gy", "gz"), None),
        ),
        out_specs=(P(None, "gx", "gy", "gz"), P(None, ("gy", "gz"))),
        check_vma=False,
    )
```

time: 70.9 us -> 67 us (0.945)
  Pallas kernels: 65.1 us -> 59.8 us
  other arithmetic: 0.33 us -> 2.16 us
    pallas_call x5 -> x1, Pallas kernels: 65.1 us -> 59.8 us  [on_device(): pl.pallas_call(functools.partial(whole_kernel, sizes), out_shape=(shape(b...]
    concatenate x2, other arithmetic: 0.15 us -> 1.37 us  [the longest x1 0.71 us: on_device(): jnp.concatenate([quad_weights[0], quad_elements[0].astype(F32)], axis=1)]
    unnamed x10 -> x9, local copies, waits for them, and re-layouts: 2.9 us -> 1.98 us
    concatenate x1 -> x0, local copies, waits for them, and re-layouts: 0.74 us -> none  [on_device(): jnp.concatenate([quad_weights[0], quad_elements[0].astype(F32)], axis=1)]
    transpose x1, local copies, waits for them, and re-layouts: 0.01 us -> 0.75 us  [on_device(): out.reshape(rp, lp, 3, pr, pw).transpose(2, 0, 3, 1, 4)]
    convert_element_type x1, other arithmetic: 0.01 us -> 0.73 us  [on_device(): quad_elements[0].astype(F32)]
where the time goes in v2:
time: 67 us; the launch traced here: 66.6 us
  Pallas kernels  59.8 us (89%)
  local copies, waits for them, and re-layouts  4.02 us (6%)
  other arithmetic  2.16 us (3%)
    pallas_call x1, Pallas kernels, on_device(): pl.pallas_call(functools.partial(whole_kernel, sizes), out_shape=(shape(b...  59.8 us
    unnamed x9, local copies, waits for them, and re-layouts  1.98 us

profile of v2, /device:TPU:0, one launch (start us, length us, event | category | flops | bytes accessed | tf_op | source)
XLA Modules:
  0.0 66.6 jit_solution(4008875824474947275)
XLA Ops:
  0.6 0.0 copy-start.1
  0.6 0.7 %convert_element_type.13 = f32[1,32,64]{2,1,0:T(8,128)S(1)} convert(s32[1,32,64]{2,1,0:T(8,128)} %param.9) | non-fusion elementwise | flops 2048 | bytes 16384 | tf_op jit(solution)/shard_map/convert_element_type | solution.py:506
  1.4 0.0 copy-done.1
  1.4 0.0 copy-start.2
  1.4 0.0 copy-start.3
  1.4 0.7 %pad_maximum_fusion.rec_in = f32[8,4,1,128]{3,2,1,0:T(1,128)} fusion(f32[8,4,1,64]{3,2,1,0:T(1,128)S(1)} %bitcast.16, f32[8,4,1,64]{3,2,1,0:T(1,128)S(1)} %bitcast.18), kind=kLoop, calls=%fused_computation.1 | loop fusion | flops 4096 | bytes 32768 | tf_op jit(solution)/shard_map/concatenate | solution.py:506
  2.1 0.0 copy-done.2
  2.1 0.0 copy-done.3
  2.1 0.1 bitcast_select_fusion
  2.2 0.0 copy-start
  2.2 0.7 pad_add_fusion.cells_in
  2.8 0.1 copy-done
  3.0 0.6 copy.11
  3.6 59.8 %shard_map.77 = (f32[4,16,16,128]{3,2,1,0:T(8,128)}, f32[2,3,8,128]{3,2,1,0:T(8,128)}) custom-call(f32[4,16,16,128]{3,2,1,0:T(8,128)} %fluid_in.1, f32[2,3,8,128]{3,2,1,0:T(8,128)} %bitcast.15, f32[8,4,1,128]{3,2,1,0:T(1,128)} %pad_maximum_fusion.rec_in, s32[16,128]{1,0:T(8,128)} %pad_add_fusion.cells_in), custom_call_target="tpu_custom_call" | custom-call | tf_op jit(solution)/shard_map/pallas_call | solution.py:532
  63.4 0.8 %copy.9 = f32[3,1,8,2,128]{4,3,2,0,1:T(2,128)S(1)} copy(f32[3,1,8,2,128]{4,2,0,3,1:T(8,128)} %bitcast.17) | data formatting | bytes 49152 | tf_op jit(solution)/shard_map/transpose | solution.py:539
  64.1 0.6 reshape.35
  64.8 1.9 %copy.13 = f32[4,16,16,128]{3,2,1,0:T(8,128)} copy(f32[4,16,16,128]{3,2,1,0:T(8,128)} %get-tuple-element.10) | data formatting | bytes 1048576
  (2 shorter events, 0.0 us)
Async XLA Ops:
  0.6 0.7 %copy-start.1 = (f32[1,32,64]{2,1,0:T(8,128)S(1)}, f32[1,32,64]{2,1,0:T(8,128)}, u32[]{:S(2)}) copy-start(f32[1,32,64]{2,1,0:T(8,128)} %param.8) | copy-start | bytes 24580
  1.4 0.7 %copy-start.2 = (s32[1,32,64]{2,1,0:T(8,128)S(1)}, s32[1,32,64]{2,1,0:T(8,128)}, u32[]{:S(2)}) copy-start(s32[1,32,64]{2,1,0:T(8,128)} %param.10) | copy-start | bytes 24580
  1.4 0.7 %copy-start.3 = (s32[1,32]{1,0:T(1,128)S(1)}, s32[1,32]{1,0:T(1,128)}, u32[]{:S(2)}) copy-start(s32[1,32]{1,0:T(1,128)} %param.11) | copy-start | bytes 388
  2.2 0.8 %copy-start = (f32[3,2048]{1,0:T(4,128)S(1)}, f32[3,2048]{1,0:T(4,128)}, u32[]{:S(2)}) copy-start(f32[3,2048]{1,0:T(4,128)} %param.7) | copy-start | bytes 73732

commit v3 on v2

--- a/solution.py
+++ b/solution.py
@@ -33,13 +33,22 @@
         z = lax.rem(self.z + d, self.nz)
         return z, (self.x, self.y, z)
 
-    def barrier(self):
+    def greet(self):
         sem = pltpu.get_barrier_semaphore()
         for d in range(1, self.plane):
             pl.semaphore_signal(sem, inc=1, device_id=self.plane_peer(d)[1], device_id_type=MESH)
         for d in range(1, self.nz):
             pl.semaphore_signal(sem, inc=1, device_id=self.line_peer(d)[1], device_id_type=MESH)
-        pl.semaphore_wait(sem, self.plane - 1 + self.nz - 1)
+        for dx in range(1, self.nx):
+            for d in range(1, self.nz):
+                pl.semaphore_signal(sem, inc=1, device_id=self.side_peer(dx, d)[1], device_id_type=MESH)
+
+    def meet(self):
+        pl.semaphore_wait(pltpu.get_barrier_semaphore(), self.plane - 1 + self.nx * (self.nz - 1))
+
+    def side_peer(self, dx, d):
+        x, z = lax.rem(self.x + dx, self.nx), lax.rem(self.z + d, self.nz)
+        return z, (x, self.y, z)
 
 
 def send(src, dst, sems, k, device):
@@ -210,42 +219,88 @@
     ]
 
 
-def gather_line(at, piece, line, sems):
-    return start_all([send(piece, line.at[at.z], sems, d - 1, at.line_peer(d)[1]) for d in range(1, at.nz)])
-
-
-def gather_plane(at, line, nodes, sems):
-    return start_all([send(line, nodes.at[at.p], sems, d - 1, at.plane_peer(d)[1]) for d in range(1, at.plane)])
-
-
-def reduce_plane(at, terms, landed, sems):
-    copies = []
-    for d in range(1, at.plane):
-        p, device = at.plane_peer(d)
-        copies.append(send(terms.at[p], landed.at[d - 1], sems, d - 1, device))
-    return start_all(copies)
-
-
-def sum_plane(at, terms, landed, sums):
-    total = terms[at.p]
-    for d in range(1, at.plane):
-        total = total + landed[d - 1]
-    sums[...] = total
-
-
-def reduce_line(at, sums, landed, sems):
-    copies = []
-    for d in range(1, at.nz):
-        z, device = at.line_peer(d)
-        copies.append(send(sums.at[z], landed.at[d - 1], sems, d - 1, device))
-    return start_all(copies)
-
-
-def sum_line(at, sums, landed):
-    total = sums[at.z]
-    for d in range(1, at.nz):
-        total = total + landed[d - 1]
-    return total
+class Gather:
+    def __init__(self, at, piece, line, nodes, sem_l, sem_p):
+        self.at, self.piece, self.line, self.nodes, self.sem_l, self.sem_p = at, piece, line, nodes, sem_l, sem_p
+        self.on_plane = []
+
+    def start(self):
+        at = self.at
+        self.on_line = start_all([
+            send(self.piece, self.line.at[at.z], self.sem_l, d - 1, at.line_peer(d)[1]) for d in range(1, at.nz)
+        ])
+        self.to_plane(0, self.piece, at.z)
+
+    def to_plane(self, k, src, z):
+        at = self.at
+        self.on_plane += start_all([
+            send(src, self.nodes.at[at.p, z], self.sem_p, k * (at.plane - 1) + d - 1, at.plane_peer(d)[1])
+            for d in range(1, at.plane)
+        ])
+
+    def forward(self):
+        at = self.at
+        for d in range(1, at.nz):
+            self.on_line[d - 1].wait_recv()
+            z = lax.rem(at.z + at.nz - d, at.nz)
+            self.to_plane(d, self.line.at[z], z)
+        self.nodes[at.p, at.z] = self.piece[...]
+        for d in range(1, at.nz):
+            z = lax.rem(at.z + at.nz - d, at.nz)
+            self.nodes[at.p, z] = self.line[z]
+
+    def wait(self):
+        for c in self.on_line:
+            c.wait_send()
+        wait_all(self.on_plane)
+
+
+class Reduce:
+    def __init__(self, at, terms, landed_p, sums, landed_l, sem_p, sem_l):
+        self.at, self.terms, self.landed_p, self.sums, self.landed_l = at, terms, landed_p, sums, landed_l
+        self.sem_p, self.sem_l = sem_p, sem_l
+        self.order = list(range(1, at.nz)) + [0]
+
+    def start(self):
+        at = self.at
+        self.on_plane = {}
+        for k in self.order:
+            z = lax.rem(at.z + k, at.nz)
+            copies = []
+            for d in range(1, at.plane):
+                p, device = at.plane_peer(d)
+                copies.append(send(self.terms.at[p, z], self.landed_p.at[k, d - 1], self.sem_p,
+                                   k * (at.plane - 1) + d - 1, device))
+            self.on_plane[k] = start_all(copies)
+
+    def forward(self, spread):
+        at = self.at
+        self.on_line = []
+        for k in self.order:
+            z = lax.rem(at.z + k, at.nz)
+            total = self.terms[at.p, z]
+            for d in range(1, at.plane):
+                self.on_plane[k][d - 1].wait_recv()
+                total = total + self.landed_p[k, d - 1]
+            self.sums[k] = total
+            for dx in range(spread):
+                if k or dx:
+                    self.on_line += start_all([
+                        send(self.sums.at[k], self.landed_l.at[dx, k], self.sem_l, dx * at.nz + k,
+                             at.side_peer(dx, k)[1])
+                    ])
+
+    def wait(self):
+        wait_all(self.on_line)
+        for copies in self.on_plane.values():
+            for c in copies:
+                c.wait_send()
+
+    def total(self, dx):
+        total = self.sums[0] if dx == 0 else self.landed_l[dx, 0]
+        for k in range(1, self.at.nz):
+            total = total + self.landed_l[dx, k]
+        return total
 
 
 class Couple:
@@ -384,100 +439,113 @@
         fluid[3, first:first + bx] = self.half[3]
 
 
-def whole_kernel(sizes, fluid_in, shell_in, rec_in, cells_in, fluid, out, *refs):
+def prepare(sizes, shell_raw, weights, elements, owned, counts, shell, rec, cells, joined, total):
+    nx, _, nz = sizes
+    pr, pw = shell.shape[2:]
+    lp = min(2, nx)
+    for g in range(nx):
+        for r in range(pr):
+            m = ((g // lp) * pr + r) * lp * pw + (g % lp) * pw
+            for c in range(3):
+                shell[g, c, r:r + 1, :] = shell_raw[c:c + 1, m:m + pw]
+    ranks, slots = weights.shape[1:]
+    joined[:, :slots] = weights[0]
+    joined[:, slots:] = elements[0].astype(F32)
+    for i in range(ranks):
+        rec[i // nz, i % nz] = joined[i:i + 1, :]
+    same = lax.broadcasted_iota(jnp.int32, (ranks, ranks), 0) == lax.broadcasted_iota(jnp.int32, (ranks, ranks), 1)
+    count = jnp.sum(jnp.where(same, counts[...].astype(F32), 0.0), axis=1, keepdims=True)
+    slot = lax.broadcasted_iota(jnp.int32, (ranks, slots), 1).astype(F32)
+    value = jnp.where(slot < count, owned[0], total)
+    cells[:, :slots] = value[:ranks // 2]
+    cells[:, slots:] = value[ranks // 2:]
+
+
+def whole_kernel(sizes, fluid_in, shell_in, weights_in, elements_in, owned_in, counts_in, fluid, out, *refs):
     refs = list(refs)
     take = lambda n: [refs.pop(0) for _ in range(n)]
-    shell, rec, cells, sem_in = take(4)
+    raw = take(5)
+    joined, shell, rec, cells, sem_in = take(5)
     line0, line1, nodes0, nodes1, rec_line, records = take(6)
     halves, terms = take(2), take(2)
     reduce0, reduce1 = take(3), take(3)
     mine, last = take(2)
     sem_nl0, sem_np0, sem_rl, sem_rp = take(4)
-    sem_ap0, sem_al0, sem_nl1, sem_np1, sem_ap1, sem_al1, sem_g = take(7)
+    sem_ap0, sem_al0, sem_nl1, sem_np1, sem_ap1, sem_al1 = take(6)
     couple_refs = take(6)
     sweep_refs = take(10), take(10)
     at = Place(sizes)
+    at.greet()
     sweeps = [Sweep(at, h, *r) for h, r in zip(halves, sweep_refs)]
-    bx = halves[0].shape[1]
-    fetches = [
-        pltpu.make_async_copy(src, dst, sem_in.at[i])
-        for i, (src, dst) in enumerate((
-            (fluid_in, sweep_refs[0][0].at[:, 1:bx + 1]), (shell_in, shell), (rec_in, rec), (cells_in, cells)))
-    ]
-    start_all(fetches)
+    _, bx, by, bz = halves[0].shape
+    pairs = [(fluid_in, sweep_refs[0][0].at[:, 1:bx + 1])]
+    pairs += list(zip((shell_in, weights_in, elements_in, owned_in, counts_in), raw))
+    fetches = start_all([pltpu.make_async_copy(src, dst, sem_in.at[i]) for i, (src, dst) in enumerate(pairs)])
     for sweep in sweeps:
         sweep.clear_ends()
-    at.barrier()
     wait_all(fetches)
+    prepare(sizes, *raw, shell, rec, cells, joined, bx * by * bz)
+    at.meet()
     first, second = sweeps
     couples = [Couple(sizes, halves[i], (nodes0, nodes1)[i], terms[i], RecordRows(records), cells, *couple_refs)
                for i in (0, 1)]
-
+    nodes = Gather(at, shell.at[at.x], line0, nodes0, sem_nl0, sem_np0)
     first.start_x()
-    node_copies = gather_line(at, shell.at[at.x], line0, sem_nl0)
     rec_copies = []
     for d in range(1, at.nz):
         z, device = at.line_peer(d)
         rec_copies.append(send(rec.at[:, z], rec_line.at[at.z], sem_rl, d - 1, device))
     start_all(rec_copies)
-    line0[at.z] = shell[at.x]
+    nodes.start()
     rec_line[at.z] = rec[:, at.z]
     first.x_then_start_y()
-    wait_all(node_copies)
-    node_copies = gather_plane(at, line0, nodes0, sem_np0)
     wait_all(rec_copies)
     rec_copies = []
     for d in range(1, at.plane):
         p, device = at.plane_peer(d)
         rec_copies.append(send(rec_line.at[:, p], records.at[at.p], sem_rp, d - 1, device))
     start_all(rec_copies)
-    nodes0[at.p] = line0[...]
+    nodes.forward()
     records[at.p] = rec_line[:, at.p]
     first.y_then_start_z()
     first.finish()
     couples[0].gather_cells()
-    wait_all(node_copies)
+    nodes.wait()
     wait_all(rec_copies)
     couples[0].nodes_to_terms()
 
-    landed_p, sums, landed_l = reduce0
-    copies = reduce_plane(at, terms[0], landed_p, sem_ap0)
+    loads = Reduce(at, terms[0], *reduce0, sem_ap0, sem_al0)
+    loads.start()
     couples[0].force_cells(second.fx, 1)
     second.start_x()
     second.x_then_start_y()
-    wait_all(copies)
-    sum_plane(at, terms[0], landed_p, sums)
-    copies = reduce_line(at, sums, landed_l, sem_al0)
+    loads.forward(1)
     second.y_then_start_z()
-    wait_all(copies)
-    fresh = shell[at.x] + relaxation * sum_line(at, sums, landed_l)
-    mine[...] = fresh
-    line1[at.z] = fresh
-    copies = gather_line(at, mine, line1, sem_nl1)
+    loads.wait()
+    mine[...] = shell[at.x] + relaxation * loads.total(0)
+    nodes = Gather(at, mine, line1, nodes1, sem_nl1, sem_np1)
+    nodes.start()
     second.finish()
-    wait_all(copies)
-    copies = gather_plane(at, line1, nodes1, sem_np1)
-    nodes1[at.p] = line1[...]
+    nodes.forward()
     couples[1].gather_cells()
-    wait_all(copies)
+    nodes.wait()
     couples[1].nodes_to_terms()
 
-    landed_p, sums, landed_l = reduce1
-    copies = reduce_plane(at, terms[1], landed_p, sem_ap1)
+    loads = Reduce(at, terms[1], *reduce1, sem_ap1, sem_al1)
+    loads.start()
     couples[1].force_cells(fluid, 0)
-    wait_all(copies)
-    sum_plane(at, terms[1], landed_p, sums)
-    copies = reduce_line(at, sums, landed_l, sem_al1)
-    wait_all(copies)
-    fresh = mine[...] + relaxation * sum_line(at, sums, landed_l)
-    last[...] = fresh
-    copies = []
-    for d in range(1, at.nx):
-        x = lax.rem(at.x + d, at.nx)
-        copies.append(send(last, out.at[at.x], sem_g, d - 1, (x, at.y, at.z)))
-    start_all(copies)
-    out[at.x] = fresh
-    wait_all(copies)
+    loads.forward(at.nx)
+    loads.wait()
+    for dx in range(at.nx):
+        x = lax.rem(at.x + at.nx - dx, at.nx)
+        last[x] = nodes1[x * at.ny + at.y, at.z] + relaxation * loads.total(dx)
+    pr, pw = shell.shape[2:]
+    lp = min(2, at.nx)
+    for g in range(at.nx):
+        for r in range(pr):
+            m = ((g // lp) * pr + r) * lp * pw + (g % lp) * pw
+            for c in range(3):
+                out[c:c + 1, m:m + pw] = last[g, c, r:r + 1, :]
 
 
 class RecordRows:
@@ -502,28 +570,27 @@
     rp = nx // lp
     pr, pw = nodes_here // lanes // rp, lanes // lp
     piece = (3, pr, pw)
-    shell = shell_disp.reshape(3, rp, pr, lp, pw).transpose(1, 3, 0, 2, 4).reshape((nx,) + piece)
-    rec = jnp.concatenate([quad_weights[0], quad_elements[0].astype(F32)], axis=1)
-    rec = rec.reshape(plane, nz, 1, 2 * slots)
-    live = jnp.arange(slots, dtype=jnp.int32)[None, :] < owner_counts[0][:, None]
-    cells = jnp.where(live, owner_cells[0], block[1] * block[2] * block[3])
-    halves = ranks // 2
-    cells = jnp.concatenate([cells[:halves], cells[halves:]], axis=1)
+    rec_shape = (plane, nz, 1, 2 * slots)
+    shell_shape = (nx,) + piece
+    i32 = lambda s: pltpu.VMEM(s, jnp.int32)
 
     shape = lambda s: jax.ShapeDtypeStruct(s, F32)
     buf = lambda s: pltpu.VMEM(s, F32)
     line = (nz,) + piece
     full = (plane,) + line
     sem = lambda n: pltpu.SemaphoreType.DMA((2, max(n, 1)))
-    reduce_scratch = [buf((plane - 1,) + line), buf(line), buf((nz - 1,) + piece)]
+    reduce_scratch = lambda spread: [buf((nz, plane - 1) + piece), buf(line), buf((spread, nz) + piece)]
     rows = ny * nz * rp * pr
     scratch = [
-        buf(shell.shape), buf(rec.shape), pltpu.VMEM(cells.shape, jnp.int32), pltpu.SemaphoreType.DMA((4,)),
-        buf(line), buf(line), buf(full), buf(full), buf((nz, plane, 1, 2 * slots)), buf((plane, nz, 1, 2 * slots)),
+        buf(shell_disp.shape), buf(quad_weights.shape), i32(quad_elements.shape), i32(owner_cells.shape),
+        i32(owner_counts.shape),
+        buf((ranks, 2 * slots)), buf(shell_shape), buf(rec_shape), i32((ranks // 2, 2 * slots)),
+        pltpu.SemaphoreType.DMA((6,)),
+        buf(line), buf(line), buf(full), buf(full), buf((nz, plane, 1, 2 * slots)), buf(rec_shape),
         buf(block), buf(block), buf(full), buf(full),
-        *reduce_scratch, *reduce_scratch, buf(piece), buf(piece),
-        sem(nz - 1), sem(plane - 1), sem(nz - 1), sem(plane - 1),
-        sem(plane - 1), sem(nz - 1), sem(nz - 1), sem(plane - 1), sem(plane - 1), sem(nz - 1), sem(nx - 1),
+        *reduce_scratch(1), *reduce_scratch(nx), buf(piece), buf(shell_shape),
+        sem(nz - 1), sem(nz * (plane - 1)), sem(nz - 1), sem(plane - 1),
+        sem(nz * (plane - 1)), sem(nz), sem(nz - 1), sem(nz * (plane - 1)), sem(nz * (plane - 1)), sem(nx * nz),
         pltpu.VMEM((6 * rows, lanes), BF16), pltpu.VMEM((6 * rows, lanes), BF16),
         buf((3 * rows, lanes)), buf((3 * rows, lanes)), buf((3 * rows, lanes)), buf((ranks // 4, 3, 4 * slots)),
         *sweep_scratch(block), *sweep_scratch(block),
@@ -531,12 +598,11 @@
     anywhere, vmem = pl.BlockSpec(memory_space=pl.ANY), pl.BlockSpec(memory_space=pltpu.VMEM)
     fluid, out = pl.pallas_call(
         functools.partial(whole_kernel, sizes),
-        out_shape=(shape(block), shape((nx,) + piece)),
-        in_specs=[anywhere] * 4, out_specs=(vmem, vmem),
+        out_shape=(shape(block), shape(shell_disp.shape)),
+        in_specs=[anywhere] * 6, out_specs=(vmem, vmem),
         scratch_shapes=scratch,
         compiler_params=pltpu.CompilerParams(collective_id=0, has_side_effects=True, vmem_limit_bytes=56 << 20),
-    )(fluid_state, shell, rec, cells)
-    out = out.reshape(rp, lp, 3, pr, pw).transpose(2, 0, 3, 1, 4).reshape(3, nodes_here)
+    )(fluid_state, shell_disp, quad_weights, quad_elements, owner_cells, owner_counts)
     return fluid, out
 
 

time: 67 us -> 61.7 us (0.921)
  other arithmetic: 2.16 us -> 0 us
  local copies, waits for them, and re-layouts: 4.02 us -> 2.49 us
  Pallas kernels: 59.8 us -> 58.4 us
    concatenate x2 -> x0, other arithmetic: 1.37 us -> none  [the longest x1 0.71 us: on_device(): jnp.concatenate([quad_weights[0], quad_elements[0].astype(F32)], axis=1)]
    pallas_call x1, Pallas kernels: 59.8 us -> 58.4 us  [on_device(): pl.pallas_call(functools.partial(whole_kernel, sizes), out_shape=(shape(b...]
    reshape x3 -> x0, local copies, waits for them, and re-layouts: 1.29 us -> none  [the longest x2 0.64 us: on_device(): shell_disp.reshape(3, rp, pr, lp, pw).transpose(1, 3, 0, 2, 4)]
    transpose x1 -> x0, local copies, waits for them, and re-layouts: 0.75 us -> none  [on_device(): out.reshape(rp, lp, 3, pr, pw).transpose(2, 0, 3, 1, 4)]
    convert_element_type x1 -> x0, other arithmetic: 0.73 us -> none  [on_device(): quad_elements[0].astype(F32)]
    unnamed x9 -> x4, local copies, waits for them, and re-layouts: 1.98 us -> 2.49 us
where the time goes in v3:
time: 61.7 us; the launch traced here: 61.6 us
  Pallas kernels  58.4 us (95%)
  local copies, waits for them, and re-layouts  2.49 us (4%)
  between operations  0.65 us (1%)
    pallas_call x1, Pallas kernels, on_device(): pl.pallas_call(functools.partial(whole_kernel, sizes), out_shape=(shape(b...  58.4 us
    unnamed x4, local copies, waits for them, and re-layouts  2.49 us

profile of v3, /device:TPU:0, one launch (start us, length us, event | category | flops | bytes accessed | tf_op | source)
XLA Modules:
  0.0 61.6 jit_solution(14177381865491883161)
XLA Ops:
  0.6 58.4 %shard_map.77 = (f32[4,16,16,128]{3,2,1,0:T(8,128)}, f32[3,2048]{1,0:T(4,128)}) custom-call(f32[4,16,16,128]{3,2,1,0:T(8,128)} %fluid_in.1, f32[3,2048]{1,0:T(4,128)} %shell_in.1, f32[1,32,64]{2,1,0:T(8,128)} %weights_in.1, s32[1,32,64]{2,1,0:T(8,128)} %elements_in.1, s32[1,32,64]{2,1,0:T(8,128)} %owned_in.1, s32[1,32]{1,0:T(1,128)} %counts_in.1), custom_call_target="tpu_custom_call" | custom-call | tf_op jit(solution)/shard_map/pallas_call | solution.py:599
  59.1 0.0 copy-start
  59.1 1.9 %copy.10 = f32[4,16,16,128]{3,2,1,0:T(8,128)} copy(f32[4,16,16,128]{3,2,1,0:T(8,128)} %get-tuple-element.4) | data formatting | bytes 1048576
  60.9 0.0 copy-done
  60.9 0.6 copy.11
Async XLA Ops:
  59.1 1.9 %copy-start = (f32[3,2048]{1,0:T(4,128)S(1)}, f32[3,2048]{1,0:T(4,128)}, u32[]{:S(2)}) copy-start(f32[3,2048]{1,0:T(4,128)} %get-tuple-element.5) | copy-start | bytes 73732

commit v4 on v3

--- a/solution.py
+++ b/solution.py
@@ -229,7 +229,9 @@
         self.on_line = start_all([
             send(self.piece, self.line.at[at.z], self.sem_l, d - 1, at.line_peer(d)[1]) for d in range(1, at.nz)
         ])
-        self.to_plane(0, self.piece, at.z)
+
+    def own(self):
+        self.to_plane(0, self.piece, self.at.z)
 
     def to_plane(self, k, src, z):
         at = self.at
@@ -469,7 +471,7 @@
     line0, line1, nodes0, nodes1, rec_line, records = take(6)
     halves, terms = take(2), take(2)
     reduce0, reduce1 = take(3), take(3)
-    mine, last = take(2)
+    mine, last, result = take(3)
     sem_nl0, sem_np0, sem_rl, sem_rp = take(4)
     sem_ap0, sem_al0, sem_nl1, sem_np1, sem_ap1, sem_al1 = take(6)
     couple_refs = take(6)
@@ -499,6 +501,7 @@
     nodes.start()
     rec_line[at.z] = rec[:, at.z]
     first.x_then_start_y()
+    nodes.own()
     wait_all(rec_copies)
     rec_copies = []
     for d in range(1, at.plane):
@@ -518,22 +521,25 @@
     loads.start()
     couples[0].force_cells(second.fx, 1)
     second.start_x()
+    loads.forward(1)
     second.x_then_start_y()
-    loads.forward(1)
-    second.y_then_start_z()
     loads.wait()
     mine[...] = shell[at.x] + relaxation * loads.total(0)
     nodes = Gather(at, mine, line1, nodes1, sem_nl1, sem_np1)
     nodes.start()
+    nodes.own()
+    second.y_then_start_z()
+    nodes.forward()
     second.finish()
-    nodes.forward()
     couples[1].gather_cells()
     nodes.wait()
     couples[1].nodes_to_terms()
 
     loads = Reduce(at, terms[1], *reduce1, sem_ap1, sem_al1)
     loads.start()
-    couples[1].force_cells(fluid, 0)
+    couples[1].force_cells(result, 0)
+    leave = pltpu.make_async_copy(result, fluid, sem_in.at[0])
+    leave.start()
     loads.forward(at.nx)
     loads.wait()
     for dx in range(at.nx):
@@ -546,6 +552,7 @@
             m = ((g // lp) * pr + r) * lp * pw + (g % lp) * pw
             for c in range(3):
                 out[c:c + 1, m:m + pw] = last[g, c, r:r + 1, :]
+    leave.wait()
 
 
 class RecordRows:
@@ -588,7 +595,7 @@
         pltpu.SemaphoreType.DMA((6,)),
         buf(line), buf(line), buf(full), buf(full), buf((nz, plane, 1, 2 * slots)), buf(rec_shape),
         buf(block), buf(block), buf(full), buf(full),
-        *reduce_scratch(1), *reduce_scratch(nx), buf(piece), buf(shell_shape),
+        *reduce_scratch(1), *reduce_scratch(nx), buf(piece), buf(shell_shape), buf(block),
         sem(nz - 1), sem(nz * (plane - 1)), sem(nz - 1), sem(plane - 1),
         sem(nz * (plane - 1)), sem(nz), sem(nz - 1), sem(nz * (plane - 1)), sem(nz * (plane - 1)), sem(nx * nz),
         pltpu.VMEM((6 * rows, lanes), BF16), pltpu.VMEM((6 * rows, lanes), BF16),
@@ -599,7 +606,7 @@
     fluid, out = pl.pallas_call(
         functools.partial(whole_kernel, sizes),
         out_shape=(shape(block), shape(shell_disp.shape)),
-        in_specs=[anywhere] * 6, out_specs=(vmem, vmem),
+        in_specs=[anywhere] * 6, out_specs=(anywhere, vmem),
         scratch_shapes=scratch,
         compiler_params=pltpu.CompilerParams(collective_id=0, has_side_effects=True, vmem_limit_bytes=56 << 20),
     )(fluid_state, shell_disp, quad_weights, quad_elements, owner_cells, owner_counts)

time: 61.7 us -> 58.9 us (0.955)
  Pallas kernels: 58.4 us -> 55.6 us
    pallas_call x1, Pallas kernels: 58.4 us -> 55.6 us  [on_device(): pl.pallas_call(functools.partial(whole_kernel, sizes), out_shape=(shape(b...]
where the time goes in v4:
time: 58.9 us; the launch traced here: 58.7 us
  Pallas kernels  55.6 us (94%)
  local copies, waits for them, and re-layouts  2.49 us (4%)
  between operations  0.65 us (1%)
    pallas_call x1, Pallas kernels, on_device(): pl.pallas_call(functools.partial(whole_kernel, sizes), out_shape=(shape(b...  55.6 us
    unnamed x4, local copies, waits for them, and re-layouts  2.49 us

profile of v4, /device:TPU:0, one launch (start us, length us, event | category | flops | bytes accessed | tf_op | source)
XLA Modules:
  0.0 58.7 jit_solution(1153150679628196828)
XLA Ops:
  0.6 55.6 %shard_map.77 = (f32[4,16,16,128]{3,2,1,0:T(8,128)}, f32[3,2048]{1,0:T(4,128)}) custom-call(f32[4,16,16,128]{3,2,1,0:T(8,128)} %fluid_in.1, f32[3,2048]{1,0:T(4,128)} %shell_in.1, f32[1,32,64]{2,1,0:T(8,128)} %weights_in.1, s32[1,32,64]{2,1,0:T(8,128)} %elements_in.1, s32[1,32,64]{2,1,0:T(8,128)} %owned_in.1, s32[1,32]{1,0:T(1,128)} %counts_in.1), custom_call_target="tpu_custom_call" | custom-call | tf_op jit(solution)/shard_map/pallas_call | solution.py:606
  56.2 0.0 copy-start
  56.2 1.9 %copy.10 = f32[4,16,16,128]{3,2,1,0:T(8,128)} copy(f32[4,16,16,128]{3,2,1,0:T(8,128)} %get-tuple-element.4) | data formatting | bytes 1048576
  58.1 0.0 copy-done
  58.1 0.6 %copy.11 = f32[3,2048]{1,0:T(4,128)} copy(f32[3,2048]{1,0:T(4,128)S(1)} %copy-done) | data formatting | bytes 49152
Async XLA Ops:
  56.2 1.9 %copy-start = (f32[3,2048]{1,0:T(4,128)S(1)}, f32[3,2048]{1,0:T(4,128)}, u32[]{:S(2)}) copy-start(f32[3,2048]{1,0:T(4,128)} %get-tuple-element.5) | copy-start | bytes 73732
